TPU v7x, 256 devices: a whole 4x4x8 slice. The times are simulated.
256 devices in a mesh: cross: 8 (over z_hi, core), strike: 32 (over z_lo, x, y).
Axes of the slice: x: 4, y: 4, z: 8 (z_hi: 4, z_lo: 2; z = z_hi * 2 + z_lo), core: 2. Of those that a mesh axis runs over, the one named last changes fastest.
Arguments:
- pressure: float32 [1024, 8, 4096], P('strike', 'cross'), may hold values from -6 to 6
- source: float32 [1024, 8, 4096], P('strike', 'cross'), may hold values from -6 to 6
- facies: int32 [1024, 8, 4096], P('strike', 'cross'), may hold values from 0 to 7
- mobility_table: float32 [8], replicated, may hold values from 0.3 to 3
Outputs:
- pressure_out: float32 [1024, 8, 4096], P('strike', 'cross')
- defect: float32 [1024, 8, 4096], P('strike', 'cross')
All inputs are finite; a program needn't handle non-finite values.
Results may differ from a plain program's by a relative error of at most 0.0003.
Values sent between devices are 32-bit elements; how exact they have to be, the bound alone decides.
No kernel may reach another device: no remote copies, remote signals or barrier semaphores. Data moves between devices by JAX's collectives and lax.ppermute only.
A program may use at most 64 MiB of HBM per device.

v0:
```python
import math

import jax
import jax.numpy as jnp
from jax import lax
from jax.sharding import PartitionSpec as P

ND = 1024
CLASSES = 8
DEFECT = 2
SWEEPS = 3


STORE = 0.5
LOW = 0.05
HIGH = 1.95


def extended(cells, sides, width):
    for axis, dim in sides:
        count = lax.axis_size(axis)
        ends = count - 1
        head = lax.slice_in_dim(cells, 0, width, axis=dim)
        tail = lax.slice_in_dim(cells, cells.shape[dim] - width, cells.shape[dim], axis=dim)
        cells = jnp.concatenate(
            [
                lax.ppermute(tail, axis, [(i, (i + 1) % count) for i in range(ends)]),
                cells,
                lax.ppermute(head, axis, [((i + 1) % count, i) for i in range(ends)]),
            ],
            axis=dim,
        )
    return cells


def chebyshev_weights(count):
    middle = 0.5 * (LOW + HIGH)
    half = 0.5 * (HIGH - LOW)
    return [
        1.0 / (middle + half * math.cos(math.pi * (2 * j + 1) / (2 * count))) for j in range(count)
    ]


def neighbour(padded, axis, offset, shape):
    starts = [1, 1, 1]
    starts[axis] = offset
    limits = [s + n for s, n in zip(starts, shape)]
    return lax.slice(padded, starts, limits)


def operate_padded(field, mobile, padded_f, padded_m):
    total = STORE * field
    for axis in range(3):
        for offset in (0, 2):
            near_f = neighbour(padded_f, axis, offset, field.shape)
            near_m = neighbour(padded_m, axis, offset, field.shape)
            total = total + 0.5 * (mobile + near_m) * (field - near_f)
    return total


def lookup(classes, table):
    base = jnp.zeros(classes.shape, jnp.float32)
    for code in range(CLASSES):
        base = jnp.where(classes == code, table[code], base)
    return base


def cosine_table():
    index = jnp.arange(ND, dtype=jnp.int32)
    phase = index[:, None] * (2 * index[None, :] + 1) % (4 * ND)
    scale = jnp.where(index == 0, math.sqrt(1.0 / ND), math.sqrt(2.0 / ND)).astype(jnp.float32)
    return scale[:, None] * jnp.cos(phase.astype(jnp.float32) * (math.pi / (2 * ND)))


def apply_table(matrix, field):
    flat = field.reshape(field.shape[0], -1)
    product = jnp.dot(
        matrix, flat, precision=lax.Precision.HIGHEST, preferred_element_type=jnp.float32
    )
    return product.reshape(field.shape)


def plane_sweeps(rhat, mref):
    omega = chebyshev_weights(SWEEPS)
    wave = jnp.arange(ND, dtype=jnp.int32).astype(jnp.float32)
    lam = (2.0 - 2.0 * jnp.cos(wave * (math.pi / ND)))[:, None, None]
    diag = STORE + mref * (lam + 4.0)
    answer = omega[0] * rhat / diag
    for step in range(1, SWEEPS):
        padded = extended(answer, (("cross", 1), ("strike", 2)), 1)
        near = (
            padded[:, :-2, 1:-1] + padded[:, 2:, 1:-1] + padded[:, 1:-1, :-2] + padded[:, 1:-1, 2:]
        )
        answer = answer + omega[step] * (rhat - (diag * answer - mref * near)) / diag
    return answer


def per_device(pressure, source, facies, mobility_table):
    table = cosine_table()
    inverse = table.T
    base = lookup(facies, mobility_table)
    field = pressure
    defect = jnp.zeros_like(pressure)
    for step in range(DEFECT):
        mobile = base * (1.0 + 0.5 * jnp.tanh(field))
        stacked = jnp.stack([field, mobile])
        rims = extended(stacked, (("cross", 2), ("strike", 1)), 1)
        rims = jnp.pad(rims, ((0, 0), (0, 0), (0, 0), (1, 1)))
        residual = source - operate_padded(field, mobile, rims[0], rims[1])
        defect = residual
        residual_cols = lax.all_to_all(residual, "strike", split_axis=2, concat_axis=0, tiled=True)
        mobile_cols = lax.all_to_all(mobile, "strike", split_axis=2, concat_axis=0, tiled=True)
        rhat = apply_table(table, residual_cols)
        mref = jnp.mean(mobile_cols, axis=0, keepdims=True)
        answer = plane_sweeps(rhat, mref)
        correction = lax.all_to_all(
            apply_table(inverse, answer), "strike", split_axis=0, concat_axis=2, tiled=True
        )
        field = field + correction
    return (field, defect)


def solution(mesh):
    in_specs = (
        P("strike", "cross", None),
        P("strike", "cross", None),
        P("strike", "cross", None),
        P(),
    )
    out_specs = (P("strike", "cross", None), P("strike", "cross", None))
    return jax.shard_map(
        per_device, mesh=mesh, in_specs=in_specs, out_specs=out_specs, check_vma=False
    )
```

profile of v0, /device:TPU:224, one launch (start us, length us, event | category | flops | bytes accessed | tf_op | source)
XLA Modules:
  0.0 584.0 jit_solution(1894249986834673856)
XLA Ops:
  2.3 7.2 %copy_bitcast_fusion = (f32[1,32,1,4096]{3,1,2,0:T(8,128)S(1)}, f32[32,1,4096]{2,0,1:T(8,128)S(1)}) fusion(f32[32,1,4096]{2,1,0:T(1,128)} %param.4, f32[]{:T(128)} %bitcast.7, f32[]{:T(128)} %bitcast.6, f32[]{:T(128)} %bitcast.5, f32[]{:T(128)} %bitcast.4, f32[]{:T(128)} %bitcast.3, f32[]{:T(128)} %bitcast.2, f32[]{:T(128)} %bitcast.1, f32[]{:T(128)} %bitcast, ...), kind=kLoop, calls=%fused_computation.163 | loop fusion | flops 2490368 | bytes 2097184
  9.6 2.8 collective-permute-start.1
  14.3 10.4 %collective-permute-done.1 = f32[2,32,1,4096]{3,1,2,0:T(8,128)S(1)} collective-permute-done((f32[2,32,1,4096]{3,1,2,0:T(8,128)S(1)}, f32[2,32,1,4096]{3,1,2,0:T(8,128)S(1)}, u32[]{:S(2)}, u32[]{:S(2)}) %collective-permute-start.1) | collective-permute-done | bytes 1048608 | tf_op jit(solution)/shard_map/ppermute | solution.py:29
  24.7 14.8 %collective-permute-done = f32[2,32,1,4096]{3,1,2,0:T(8,128)S(1)} collective-permute-done((f32[2,32,1,4096]{3,1,2,0:T(8,128)S(1)}, f32[2,32,1,4096]{3,1,2,0:T(8,128)S(1)}, u32[]{:S(2)}, u32[]{:S(2)}) %collective-permute-start) | collective-permute-done | bytes 1048608 | tf_op jit(solution)/shard_map/ppermute | solution.py:27
  39.7 3.5 collective-permute-start.2
  43.2 7.2 %collective-permute-start.3 = (f32[2,1,3,4096]{3,1,2,0:T(1,128)S(1)}, f32[2,1,3,4096]{3,1,2,0:T(1,128)S(1)}, u32[]{:S(2)}, u32[]{:S(2)}) collective-permute-start(f32[2,1,3,4096]{3,1,2,0:T(1,128)S(1)} %get-tuple-element.21), channel_id=1, source_target_pairs={{1,0},{2,1},{3,2},{4,3},{5,4},{6,5},{7,6},{8,7},{9,8},{10,9},{11,1... | collective-permute-start | bytes 294920 | tf_op jit(solution)/shard_map/ppermute | solution.py:29
  50.4 2.5 copy.185
  53.4 19.2 %reduce.14 = f32[4096,32]{1,0:T(8,128)} reduce(f32[4096,1,32]{2,1,0:T(1,128)S(1)} %bitcast.96, f32[]{:T(128)} %broadcast.264), dimensions={1}, to_apply=%bitcast.75.reduce_sub_computation | reduce | bytes 1048580
  72.6 3.3 reshape.183
  75.9 4.9 all-to-all-start.1
  80.8 3.5 select_maximum_fusion.5
  85.5 2.4 fusion.68
  87.9 4.7 copy.182
  92.6 19.3 %reduce.12 = f32[4096,32]{1,0:T(8,128)} reduce(f32[4096,1,32]{2,1,0:T(1,128)S(1)} %bitcast.97, f32[]{:T(128)} %broadcast.264), dimensions={1}, to_apply=%bitcast.73.reduce_sub_computation | reduce | bytes 1048580
  111.9 3.1 reshape.181
  115.0 9.0 %all-to-all-start = ((f32[32,1,4096]{2,1,0:T(1,128)}), f32[32,1,4096]{2,1,0:T(1,128)}, u32[]{:S(2)}, u32[]{:S(2)}) async-start(f32[32,1,4096]{2,1,0:T(1,128)} %reshape.181), calls=%async_computation | async-start | bytes 1048576 | tf_op jit(solution)/shard_map/all_to_all | solution.py:111
  124.0 2.9 reduce.15
  126.9 3.5 reshape.184
  130.4 30.5 %bitcast_reduce_fusion.3 = f32[4096]{0:T(1024)S(1)} fusion(f32[4096,1,32]{2,1,0:T(1,128)S(1)} %reshape.184), kind=kLoop, calls=%fused_computation.226 | loop fusion | flops 126976 | bytes 540672 | tf_op jit(solution)/shard_map/reduce_sum | solution.py:114
  160.9 2.9 reduce.13
  163.7 3.5 reshape.182
  168.9 19.3 %fusion.15 = f32[1024,128]{0,1:T(8,128)S(1)} fusion(f32[1024,128]{1,0:T(8,128)S(1)} %bitcast.107, s32[1024]{0:T(1024)S(1)} %multiply_add_fusion.4, f32[1024]{0:T(1024)S(1)} %get-tuple-element.41), kind=kOutput, calls=%fused_computation.27 | convolution fusion | flops 1626341376 | bytes 1056768 | tf_op jit(solution)/shard_map/dot_general | solution.py:77
  190.3 2.4 collective-permute-start.4
  192.7 4.3 collective-permute-done.5
  197.0 9.8 %collective-permute-done.4 = f32[1024,1,128]{0,2,1:T(8,128)S(1)} collective-permute-done((f32[1024,1,128]{0,2,1:T(8,128)S(1)}, f32[1024,1,128]{0,2,1:T(8,128)S(1)}, u32[]{:S(2)}, u32[]{:S(2)}) %collective-permute-start.4) | collective-permute-done | bytes 524320 | tf_op jit(solution)/shard_map/ppermute | solution.py:27
  206.9 3.8 collective-permute-start.6
  210.7 6.3 %collective-permute-start.7 = (f32[1024,3,1]{0,2,1:T(1,128)S(1)}, f32[1024,3,1]{0,2,1:T(1,128)S(1)}, u32[]{:S(2)}, u32[]{:S(2)}) collective-permute-start(f32[1024,3,1]{0,2,1:T(1,128)S(1)} %get-tuple-element.29), channel_id=1, source_target_pairs={{1,0},{2,1},{3,2},{4,3},{5,4},{6,5},{7,6},{8,7},{9,8},{10,9},{11,1... | collective-permute-start | bytes 36872 | tf_op jit(solution)/shard_map/ppermute | solution.py:29
  220.8 2.4 collective-permute-start.8
  223.2 4.2 collective-permute-done.9
  227.4 8.6 %collective-permute-done.8 = f32[1024,1,128]{0,2,1:T(8,128)S(1)} collective-permute-done((f32[1024,1,128]{0,2,1:T(8,128)S(1)}, f32[1024,1,128]{0,2,1:T(8,128)S(1)}, u32[]{:S(2)}, u32[]{:S(2)}) %collective-permute-start.8) | collective-permute-done | bytes 524320 | tf_op jit(solution)/shard_map/ppermute | solution.py:27
  238.1 8.3 %collective-permute-start.11 = (f32[1024,3,1]{0,2,1:T(1,128)S(1)}, f32[1024,3,1]{0,2,1:T(1,128)S(1)}, u32[]{:S(2)}, u32[]{:S(2)}) collective-permute-start(f32[1024,3,1]{0,2,1:T(1,128)S(1)} %get-tuple-element.27), channel_id=1, source_target_pairs={{1,0},{2,1},{3,2},{4,3},{5,4},{6,5},{7,6},{8,7},{9,8},{10,9},{11,1... | collective-permute-start | bytes 36872 | tf_op jit(solution)/shard_map/ppermute | solution.py:29
  247.7 22.9 %fusion.13 = f32[1024,128]{1,0:T(8,128)S(1)} fusion(s32[1024]{0:T(1024)S(1)} %multiply_add_fusion.4, f32[1024]{0:T(1024)S(1)} %get-tuple-element.41, f32[1024,1,128]{0,2,1:T(8,128)S(1)} %fusion.64, f32[1024,3,1]{0,2,1:T(1,128)S(1)} %collective-permute-done.11, f32[1024,1,128]{0,2,1:T(8,128)S(1)} %collective-permute-done.9, ...), kind=kOutput, calls=%fused_computation.26 | convolution fusion | flops 1628700672 | bytes 2658816 | tf_op jit(solution)/shard_map/dot_general | solution.py:77
  270.6 17.9 %all_to_all.84 = f32[1024,1,128]{2,1,0:T(1,128)S(1)} all-to-all(f32[1024,1,128]{2,1,0:T(1,128)S(1)} %bitcast.106), channel_id=1, replica_groups=mesh['cross'=8,'strike'=32] {'strike'}, dimensions={0} | all-to-all | bytes 1048576 | tf_op jit(solution)/shard_map/all_to_all | solution.py:116
  288.9 6.4 %add_multiply_fusion = (f32[32,1,4096]{2,0,1:T(8,128)S(1)}, f32[32,1,4096]{2,0,1:T(8,128)S(1)}) fusion(f32[]{:T(128)} %bitcast.7, f32[]{:T(128)} %bitcast.6, f32[]{:T(128)} %bitcast.5, f32[]{:T(128)} %bitcast.4, f32[]{:T(128)} %bitcast.3, f32[]{:T(128)} %bitcast.2, f32[]{:T(128)} %bitcast.1, f32[]{:T(128)} %bitcast, s32[32,1,4096]{2,1,0:T(1,128)S(1)} %copy-done.9, ...), kind=kLoop, calls=%fused_computation.157 | loop fusion | flops 2621440 | bytes 2621472 | tf_op jit(solution)/shard_map/mul | solution.py:105
  297.3 2.5 collective-permute-start.12
  299.8 9.9 %collective-permute-done.13 = f32[2,32,1,4096]{3,1,2,0:T(8,128)S(1)} collective-permute-done((f32[2,32,1,4096]{3,1,2,0:T(8,128)S(1)}, f32[2,32,1,4096]{3,1,2,0:T(8,128)S(1)}, u32[]{:S(2)}, u32[]{:S(2)}) %collective-permute-start.13) | collective-permute-done | bytes 1048608 | tf_op jit(solution)/shard_map/ppermute | solution.py:29
  309.6 12.6 %collective-permute-done.12 = f32[2,32,1,4096]{3,1,2,0:T(8,128)S(1)} collective-permute-done((f32[2,32,1,4096]{3,1,2,0:T(8,128)S(1)}, f32[2,32,1,4096]{3,1,2,0:T(8,128)S(1)}, u32[]{:S(2)}, u32[]{:S(2)}) %collective-permute-start.12) | collective-permute-done | bytes 1048608 | tf_op jit(solution)/shard_map/ppermute | solution.py:27
  325.1 9.1 %collective-permute-start.15 = (f32[2,1,3,4096]{3,1,2,0:T(1,128)S(1)}, f32[2,1,3,4096]{3,1,2,0:T(1,128)S(1)}, u32[]{:S(2)}, u32[]{:S(2)}) collective-permute-start(f32[2,1,3,4096]{3,1,2,0:T(1,128)S(1)} %get-tuple-element.19), channel_id=1, source_target_pairs={{1,0},{2,1},{3,2},{4,3},{5,4},{6,5},{7,6},{8,7},{9,8},{10,9},{11,1... | collective-permute-start | bytes 294920 | tf_op jit(solution)/shard_map/ppermute | solution.py:29
  334.2 3.7 copy.194
  337.9 19.0 %reduce.18 = f32[4096,32]{1,0:T(8,128)S(1)} reduce(f32[4096,1,32]{2,1,0:T(1,128)} %bitcast.98, f32[]{:T(128)} %broadcast.264), dimensions={1}, to_apply=%bitcast.79.reduce_sub_computation | reduce | bytes 1048580
  358.6 6.9 %all-to-all-start.4 = ((f32[32,1,4096]{2,1,0:T(1,128)}), f32[32,1,4096]{2,1,0:T(1,128)}, u32[]{:S(2)}, u32[]{:S(2)}) async-start(f32[32,1,4096]{2,1,0:T(1,128)} %reshape.187), calls=%async_computation.4 | async-start | bytes 1048576 | tf_op jit(solution)/shard_map/all_to_all | solution.py:112
  365.5 4.7 select_maximum_fusion
  372.8 3.6 copy.191
  376.4 19.0 %reduce.16 = f32[4096,32]{1,0:T(8,128)S(1)} reduce(f32[4096,1,32]{2,1,0:T(1,128)} %bitcast.99, f32[]{:T(128)} %broadcast.264), dimensions={1}, to_apply=%bitcast.77.reduce_sub_computation | reduce | bytes 1048580
  397.1 9.0 %all-to-all-start.3 = ((f32[32,1,4096]{2,1,0:T(1,128)}), f32[32,1,4096]{2,1,0:T(1,128)}, u32[]{:S(2)}, u32[]{:S(2)}) async-start(f32[32,1,4096]{2,1,0:T(1,128)} %reshape.185), calls=%async_computation.3 | async-start | bytes 1048576 | tf_op jit(solution)/shard_map/all_to_all | solution.py:111
  406.1 3.6 reduce.19
  409.8 4.5 reshape.188
  414.3 30.5 %bitcast_reduce_fusion.2 = f32[4096]{0:T(1024)S(1)} fusion(f32[4096,1,32]{2,1,0:T(1,128)S(1)} %reshape.188), kind=kLoop, calls=%fused_computation.225 | loop fusion | flops 126976 | bytes 540672 | tf_op jit(solution)/shard_map/reduce_sum | solution.py:114
  444.8 3.6 reduce.17
  448.5 4.5 reshape.186
  453.0 3.3 copy.192
  457.7 19.3 %fusion.11 = f32[1024,128]{0,1:T(8,128)S(1)} fusion(f32[1024,128]{1,0:T(8,128)S(1)} %bitcast.108, s32[1024]{0:T(1024)S(1)} %multiply_add_fusion.4, f32[1024]{0:T(1024)S(1)} %get-tuple-element.41), kind=kOutput, calls=%fused_computation.25 | convolution fusion | flops 1626341376 | bytes 1056768 | tf_op jit(solution)/shard_map/dot_general | solution.py:77
  479.0 2.4 collective-permute-start.16
  481.5 4.3 collective-permute-done.17
  485.8 12.8 %collective-permute-done.16 = f32[1024,1,128]{0,2,1:T(8,128)S(1)} collective-permute-done((f32[1024,1,128]{0,2,1:T(8,128)S(1)}, f32[1024,1,128]{0,2,1:T(8,128)S(1)}, u32[]{:S(2)}, u32[]{:S(2)}) %collective-permute-start.16) | collective-permute-done | bytes 524320 | tf_op jit(solution)/shard_map/ppermute | solution.py:27
  498.6 3.8 collective-permute-start.18
  502.4 6.3 %collective-permute-start.19 = (f32[1024,3,1]{0,2,1:T(1,128)S(1)}, f32[1024,3,1]{0,2,1:T(1,128)S(1)}, u32[]{:S(2)}, u32[]{:S(2)}) collective-permute-start(f32[1024,3,1]{0,2,1:T(1,128)S(1)} %get-tuple-element.25), channel_id=1, source_target_pairs={{1,0},{2,1},{3,2},{4,3},{5,4},{6,5},{7,6},{8,7},{9,8},{10,9},{11,1... | collective-permute-start | bytes 36872 | tf_op jit(solution)/shard_map/ppermute | solution.py:29
  512.4 2.4 collective-permute-start.20
  514.9 4.2 collective-permute-done.21
  519.1 6.3 %collective-permute-done.20 = f32[1024,1,128]{0,2,1:T(8,128)S(1)} collective-permute-done((f32[1024,1,128]{0,2,1:T(8,128)S(1)}, f32[1024,1,128]{0,2,1:T(8,128)S(1)}, u32[]{:S(2)}, u32[]{:S(2)}) %collective-permute-start.20) | collective-permute-done | bytes 524320 | tf_op jit(solution)/shard_map/ppermute | solution.py:27
  527.8 11.0 %collective-permute-start.23 = (f32[1024,3,1]{0,2,1:T(1,128)S(1)}, f32[1024,3,1]{0,2,1:T(1,128)S(1)}, u32[]{:S(2)}, u32[]{:S(2)}) collective-permute-start(f32[1024,3,1]{0,2,1:T(1,128)S(1)} %get-tuple-element.23), channel_id=1, source_target_pairs={{1,0},{2,1},{3,2},{4,3},{5,4},{6,5},{7,6},{8,7},{9,8},{10,9},{11,1... | collective-permute-start | bytes 36872 | tf_op jit(solution)/shard_map/ppermute | solution.py:29
  540.2 23.5 %fusion.9 = f32[1024,128]{1,0:T(8,128)} fusion(s32[1024]{0:T(1024)S(1)} %multiply_add_fusion.4, f32[1024]{0:T(1024)S(1)} %get-tuple-element.41, f32[1024,1,128]{0,2,1:T(8,128)S(1)} %fusion.30, f32[1024,3,1]{0,2,1:T(1,128)S(1)} %collective-permute-done.23, f32[1024,1,128]{0,2,1:T(8,128)S(1)} %collective-permute-done.21, ...), kind=kOutput, calls=%fused_computation.24 | convolution fusion | flops 1628700672 | bytes 2658816 | tf_op jit(solution)/shard_map/dot_general | solution.py:77
  563.6 8.5 %all-to-all-start.5 = ((f32[1024,1,128]{2,1,0:T(1,128)}), f32[1024,1,128]{2,1,0:T(1,128)S(1)}, u32[]{:S(2)}, u32[]{:S(2)}) async-start(f32[1024,1,128]{2,1,0:T(1,128)} %bitcast.37), calls=%async_computation.5 | async-start | bytes 1048576 | tf_op jit(solution)/shard_map/all_to_all | solution.py:116
  573.5 8.1 %all-to-all-done.5 = f32[1024,1,128]{2,1,0:T(1,128)S(1)} async-done(((f32[1024,1,128]{2,1,0:T(1,128)}), f32[1024,1,128]{2,1,0:T(1,128)S(1)}, u32[]{:S(2)}, u32[]{:S(2)}) %all-to-all-start.5) | async-done | bytes 524320 | tf_op jit(solution)/shard_map/all_to_all | solution.py:116
  (78 shorter events, 42.0 us)
Async XLA Ops:
  9.6 15.1 %collective-permute-start.1 = (f32[2,32,1,4096]{3,1,2,0:T(8,128)S(1)}, f32[2,32,1,4096]{3,1,2,0:T(8,128)S(1)}, u32[]{:S(2)}, u32[]{:S(2)}) collective-permute-start(f32[2,32,1,4096]{3,1,2,0:T(8,128)S(1)} %pad_maximum_fusion), channel_id=1, source_target_pairs={{32,0},{64,32},{96,64},{128,96},{160,128},{192,160},{224,192},{33,... | collective-permute-start | bytes 3145736 | tf_op jit(solution)/shard_map/ppermute | solution.py:29
  12.4 27.1 %collective-permute-start = (f32[2,32,1,4096]{3,1,2,0:T(8,128)S(1)}, f32[2,32,1,4096]{3,1,2,0:T(8,128)S(1)}, u32[]{:S(2)}, u32[]{:S(2)}) collective-permute-start(f32[2,32,1,4096]{3,1,2,0:T(8,128)S(1)} %pad_maximum_fusion), channel_id=1, source_target_pairs={{0,32},{32,64},{64,96},{96,128},{128,160},{160,192},{192,224},{1,3... | collective-permute-start | bytes 3145736 | tf_op jit(solution)/shard_map/ppermute | solution.py:27
  24.7 18.5 %copy-start.1 = (f32[2,32,1,4096]{3,1,2,0:T(8,128)}, f32[2,32,1,4096]{3,1,2,0:T(8,128)S(1)}, u32[]{:S(2)}) copy-start(f32[2,32,1,4096]{3,1,2,0:T(8,128)S(1)} %collective-permute-done.1) | copy-start | bytes 3145732
  39.5 3.7 copy-start.3
  39.7 41.1 %collective-permute-start.2 = (f32[2,1,3,4096]{3,1,2,0:T(1,128)S(1)}, f32[2,1,3,4096]{3,1,2,0:T(1,128)S(1)}, u32[]{:S(2)}, u32[]{:S(2)}) collective-permute-start(f32[2,1,3,4096]{3,1,2,0:T(1,128)S(1)} %get-tuple-element.20), channel_id=1, source_target_pairs={{0,1},{1,2},{2,3},{3,4},{4,5},{5,6},{6,7},{7,8},{8,9},{9,10},{10,1... | collective-permute-start | bytes 294920 | tf_op jit(solution)/shard_map/ppermute | solution.py:27
  43.2 37.6 %collective-permute-start.3 = (f32[2,1,3,4096]{3,1,2,0:T(1,128)S(1)}, f32[2,1,3,4096]{3,1,2,0:T(1,128)S(1)}, u32[]{:S(2)}, u32[]{:S(2)}) collective-permute-start(f32[2,1,3,4096]{3,1,2,0:T(1,128)S(1)} %get-tuple-element.21), channel_id=1, source_target_pairs={{1,0},{2,1},{3,2},{4,3},{5,4},{6,5},{7,6},{8,7},{9,8},{10,9},{11,1... | collective-permute-start | bytes 294920 | tf_op jit(solution)/shard_map/ppermute | solution.py:29
  72.6 8.2 %copy-start.2 = (f32[2,32,1,4096]{3,1,2,0:T(8,128)S(1)}, f32[2,32,1,4096]{3,1,2,0:T(8,128)}, u32[]{:S(2)}) copy-start(f32[2,32,1,4096]{3,1,2,0:T(8,128)} %copy-done.1) | copy-start | bytes 3145732
  72.6 8.2 %copy-start.4 = (f32[2,32,1,4096]{3,1,2,0:T(8,128)S(1)}, f32[2,32,1,4096]{3,1,2,0:T(8,128)}, u32[]{:S(2)}) copy-start(f32[2,32,1,4096]{3,1,2,0:T(8,128)} %copy-done.3) | copy-start | bytes 3145732
  75.9 39.1 %all-to-all-start.1 = ((f32[32,1,4096]{2,1,0:T(1,128)}), f32[32,1,4096]{2,1,0:T(1,128)}, u32[]{:S(2)}, u32[]{:S(2)}) async-start(f32[32,1,4096]{2,1,0:T(1,128)} %reshape.183), calls=%async_computation.1 | async-start | bytes 1048576 | tf_op jit(solution)/shard_map/all_to_all | solution.py:112
  84.3 1.0 copy-start
  84.3 1.2 copy-start.7
  115.0 45.9 %all-to-all-start = ((f32[32,1,4096]{2,1,0:T(1,128)}), f32[32,1,4096]{2,1,0:T(1,128)}, u32[]{:S(2)}, u32[]{:S(2)}) async-start(f32[32,1,4096]{2,1,0:T(1,128)} %reshape.181), calls=%async_computation | async-start | bytes 1048576 | tf_op jit(solution)/shard_map/all_to_all | solution.py:111
  188.4 8.7 %collective-permute-start.5 = (f32[1024,1,128]{0,2,1:T(8,128)S(1)}, f32[1024,1,128]{0,2,1:T(8,128)S(1)}, u32[]{:S(2)}, u32[]{:S(2)}) collective-permute-start(f32[1024,1,128]{0,2,1:T(8,128)S(1)} %fusion.91), channel_id=1, source_target_pairs={{32,0},{64,32},{96,64},{128,96},{160,128},{192,160},{224,192},{33,... | collective-permute-start | bytes 1572872 | tf_op jit(solution)/shard_map/ppermute | solution.py:29
  190.3 16.6 %collective-permute-start.4 = (f32[1024,1,128]{0,2,1:T(8,128)S(1)}, f32[1024,1,128]{0,2,1:T(8,128)S(1)}, u32[]{:S(2)}, u32[]{:S(2)}) collective-permute-start(f32[1024,1,128]{0,2,1:T(8,128)S(1)} %fusion.91), channel_id=1, source_target_pairs={{0,32},{32,64},{64,96},{96,128},{128,160},{160,192},{192,224},{1,3... | collective-permute-start | bytes 1572872 | tf_op jit(solution)/shard_map/ppermute | solution.py:27
  206.9 10.1 %collective-permute-start.6 = (f32[1024,3,1]{0,2,1:T(1,128)S(1)}, f32[1024,3,1]{0,2,1:T(1,128)S(1)}, u32[]{:S(2)}, u32[]{:S(2)}) collective-permute-start(f32[1024,3,1]{0,2,1:T(1,128)S(1)} %get-tuple-element.28), channel_id=1, source_target_pairs={{0,1},{1,2},{2,3},{3,4},{4,5},{5,6},{6,7},{7,8},{8,9},{9,10},{10,1... | collective-permute-start | bytes 36872 | tf_op jit(solution)/shard_map/ppermute | solution.py:27
  210.7 7.6 %collective-permute-start.7 = (f32[1024,3,1]{0,2,1:T(1,128)S(1)}, f32[1024,3,1]{0,2,1:T(1,128)S(1)}, u32[]{:S(2)}, u32[]{:S(2)}) collective-permute-start(f32[1024,3,1]{0,2,1:T(1,128)S(1)} %get-tuple-element.29), channel_id=1, source_target_pairs={{1,0},{2,1},{3,2},{4,3},{5,4},{6,5},{7,6},{8,7},{9,8},{10,9},{11,1... | collective-permute-start | bytes 36872 | tf_op jit(solution)/shard_map/ppermute | solution.py:29
  218.8 8.6 %collective-permute-start.9 = (f32[1024,1,128]{0,2,1:T(8,128)S(1)}, f32[1024,1,128]{0,2,1:T(8,128)S(1)}, u32[]{:S(2)}, u32[]{:S(2)}) collective-permute-start(f32[1024,1,128]{0,2,1:T(8,128)S(1)} %fusion.64), channel_id=1, source_target_pairs={{32,0},{64,32},{96,64},{128,96},{160,128},{192,160},{224,192},{33,... | collective-permute-start | bytes 1572872 | tf_op jit(solution)/shard_map/ppermute | solution.py:29
  220.8 15.3 %collective-permute-start.8 = (f32[1024,1,128]{0,2,1:T(8,128)S(1)}, f32[1024,1,128]{0,2,1:T(8,128)S(1)}, u32[]{:S(2)}, u32[]{:S(2)}) collective-permute-start(f32[1024,1,128]{0,2,1:T(8,128)S(1)} %fusion.64), channel_id=1, source_target_pairs={{0,32},{32,64},{64,96},{96,128},{128,160},{160,192},{192,224},{1,3... | collective-permute-start | bytes 1572872 | tf_op jit(solution)/shard_map/ppermute | solution.py:27
  236.1 10.2 %collective-permute-start.10 = (f32[1024,3,1]{0,2,1:T(1,128)S(1)}, f32[1024,3,1]{0,2,1:T(1,128)S(1)}, u32[]{:S(2)}, u32[]{:S(2)}) collective-permute-start(f32[1024,3,1]{0,2,1:T(1,128)S(1)} %get-tuple-element.26), channel_id=1, source_target_pairs={{0,1},{1,2},{2,3},{3,4},{4,5},{5,6},{6,7},{7,8},{8,9},{9,10},{10,1... | collective-permute-start | bytes 36872 | tf_op jit(solution)/shard_map/ppermute | solution.py:27
  238.0 50.8 %copy-start.9 = (s32[32,1,4096]{2,1,0:T(1,128)S(1)}, s32[32,1,4096]{2,1,0:T(1,128)}, u32[]{:S(2)}) copy-start(s32[32,1,4096]{2,1,0:T(1,128)} %param.6) | copy-start | bytes 1572868
  238.1 9.7 %collective-permute-start.11 = (f32[1024,3,1]{0,2,1:T(1,128)S(1)}, f32[1024,3,1]{0,2,1:T(1,128)S(1)}, u32[]{:S(2)}, u32[]{:S(2)}) collective-permute-start(f32[1024,3,1]{0,2,1:T(1,128)S(1)} %get-tuple-element.27), channel_id=1, source_target_pairs={{1,0},{2,1},{3,2},{4,3},{5,4},{6,5},{7,6},{8,7},{9,8},{10,9},{11,1... | collective-permute-start | bytes 36872 | tf_op jit(solution)/shard_map/ppermute | solution.py:29
  295.4 14.3 %collective-permute-start.13 = (f32[2,32,1,4096]{3,1,2,0:T(8,128)S(1)}, f32[2,32,1,4096]{3,1,2,0:T(8,128)S(1)}, u32[]{:S(2)}, u32[]{:S(2)}) collective-permute-start(f32[2,32,1,4096]{3,1,2,0:T(8,128)S(1)} %pad_maximum_fusion.1), channel_id=1, source_target_pairs={{32,0},{64,32},{96,64},{128,96},{160,128},{192,160},{224,192},{33,... | collective-permute-start | bytes 3145736 | tf_op jit(solution)/shard_map/ppermute | solution.py:29
  297.3 24.9 %collective-permute-start.12 = (f32[2,32,1,4096]{3,1,2,0:T(8,128)S(1)}, f32[2,32,1,4096]{3,1,2,0:T(8,128)S(1)}, u32[]{:S(2)}, u32[]{:S(2)}) collective-permute-start(f32[2,32,1,4096]{3,1,2,0:T(8,128)S(1)} %pad_maximum_fusion.1), channel_id=1, source_target_pairs={{0,32},{32,64},{64,96},{96,128},{128,160},{160,192},{192,224},{1,3... | collective-permute-start | bytes 3145736 | tf_op jit(solution)/shard_map/ppermute | solution.py:27
  309.6 12.6 %copy-start.5 = (f32[2,32,1,4096]{3,1,2,0:T(8,128)}, f32[2,32,1,4096]{3,1,2,0:T(8,128)S(1)}, u32[]{:S(2)}) copy-start(f32[2,32,1,4096]{3,1,2,0:T(8,128)S(1)} %collective-permute-done.13) | copy-start | bytes 3145732
  322.2 1.0 copy-start.6
  323.2 42.2 %collective-permute-start.14 = (f32[2,1,3,4096]{3,1,2,0:T(1,128)S(1)}, f32[2,1,3,4096]{3,1,2,0:T(1,128)S(1)}, u32[]{:S(2)}, u32[]{:S(2)}) collective-permute-start(f32[2,1,3,4096]{3,1,2,0:T(1,128)S(1)} %get-tuple-element.18), channel_id=1, source_target_pairs={{0,1},{1,2},{2,3},{3,4},{4,5},{5,6},{6,7},{7,8},{8,9},{9,10},{10,1... | collective-permute-start | bytes 294920 | tf_op jit(solution)/shard_map/ppermute | solution.py:27
  325.1 40.3 %collective-permute-start.15 = (f32[2,1,3,4096]{3,1,2,0:T(1,128)S(1)}, f32[2,1,3,4096]{3,1,2,0:T(1,128)S(1)}, u32[]{:S(2)}, u32[]{:S(2)}) collective-permute-start(f32[2,1,3,4096]{3,1,2,0:T(1,128)S(1)} %get-tuple-element.19), channel_id=1, source_target_pairs={{1,0},{2,1},{3,2},{4,3},{5,4},{6,5},{7,6},{8,7},{9,8},{10,9},{11,1... | collective-permute-start | bytes 294920 | tf_op jit(solution)/shard_map/ppermute | solution.py:29
  358.6 38.6 %all-to-all-start.4 = ((f32[32,1,4096]{2,1,0:T(1,128)}), f32[32,1,4096]{2,1,0:T(1,128)}, u32[]{:S(2)}, u32[]{:S(2)}) async-start(f32[32,1,4096]{2,1,0:T(1,128)} %reshape.187), calls=%async_computation.4 | async-start | bytes 1048576 | tf_op jit(solution)/shard_map/all_to_all | solution.py:112
  370.1 1.0 copy-start.8
  397.1 47.7 %all-to-all-start.3 = ((f32[32,1,4096]{2,1,0:T(1,128)}), f32[32,1,4096]{2,1,0:T(1,128)}, u32[]{:S(2)}, u32[]{:S(2)}) async-start(f32[32,1,4096]{2,1,0:T(1,128)} %reshape.185), calls=%async_computation.3 | async-start | bytes 1048576 | tf_op jit(solution)/shard_map/all_to_all | solution.py:111
  477.1 8.7 %collective-permute-start.17 = (f32[1024,1,128]{0,2,1:T(8,128)S(1)}, f32[1024,1,128]{0,2,1:T(8,128)S(1)}, u32[]{:S(2)}, u32[]{:S(2)}) collective-permute-start(f32[1024,1,128]{0,2,1:T(8,128)S(1)} %fusion.92), channel_id=1, source_target_pairs={{32,0},{64,32},{96,64},{128,96},{160,128},{192,160},{224,192},{33,... | collective-permute-start | bytes 1572872 | tf_op jit(solution)/shard_map/ppermute | solution.py:29
  479.0 19.5 %collective-permute-start.16 = (f32[1024,1,128]{0,2,1:T(8,128)S(1)}, f32[1024,1,128]{0,2,1:T(8,128)S(1)}, u32[]{:S(2)}, u32[]{:S(2)}) collective-permute-start(f32[1024,1,128]{0,2,1:T(8,128)S(1)} %fusion.92), channel_id=1, source_target_pairs={{0,32},{32,64},{64,96},{96,128},{128,160},{160,192},{192,224},{1,3... | collective-permute-start | bytes 1572872 | tf_op jit(solution)/shard_map/ppermute | solution.py:27
  498.6 10.1 %collective-permute-start.18 = (f32[1024,3,1]{0,2,1:T(1,128)S(1)}, f32[1024,3,1]{0,2,1:T(1,128)S(1)}, u32[]{:S(2)}, u32[]{:S(2)}) collective-permute-start(f32[1024,3,1]{0,2,1:T(1,128)S(1)} %get-tuple-element.24), channel_id=1, source_target_pairs={{0,1},{1,2},{2,3},{3,4},{4,5},{5,6},{6,7},{7,8},{8,9},{9,10},{10,1... | collective-permute-start | bytes 36872 | tf_op jit(solution)/shard_map/ppermute | solution.py:27
  502.4 7.6 %collective-permute-start.19 = (f32[1024,3,1]{0,2,1:T(1,128)S(1)}, f32[1024,3,1]{0,2,1:T(1,128)S(1)}, u32[]{:S(2)}, u32[]{:S(2)}) collective-permute-start(f32[1024,3,1]{0,2,1:T(1,128)S(1)} %get-tuple-element.25), channel_id=1, source_target_pairs={{1,0},{2,1},{3,2},{4,3},{5,4},{6,5},{7,6},{8,7},{9,8},{10,9},{11,1... | collective-permute-start | bytes 36872 | tf_op jit(solution)/shard_map/ppermute | solution.py:29
  510.5 8.6 %collective-permute-start.21 = (f32[1024,1,128]{0,2,1:T(8,128)S(1)}, f32[1024,1,128]{0,2,1:T(8,128)S(1)}, u32[]{:S(2)}, u32[]{:S(2)}) collective-permute-start(f32[1024,1,128]{0,2,1:T(8,128)S(1)} %fusion.30), channel_id=1, source_target_pairs={{32,0},{64,32},{96,64},{128,96},{160,128},{192,160},{224,192},{33,... | collective-permute-start | bytes 1572872 | tf_op jit(solution)/shard_map/ppermute | solution.py:29
  512.4 13.0 %collective-permute-start.20 = (f32[1024,1,128]{0,2,1:T(8,128)S(1)}, f32[1024,1,128]{0,2,1:T(8,128)S(1)}, u32[]{:S(2)}, u32[]{:S(2)}) collective-permute-start(f32[1024,1,128]{0,2,1:T(8,128)S(1)} %fusion.30), channel_id=1, source_target_pairs={{0,32},{32,64},{64,96},{96,128},{128,160},{160,192},{192,224},{1,3... | collective-permute-start | bytes 1572872 | tf_op jit(solution)/shard_map/ppermute | solution.py:27
  525.5 13.3 %collective-permute-start.22 = (f32[1024,3,1]{0,2,1:T(1,128)S(1)}, f32[1024,3,1]{0,2,1:T(1,128)S(1)}, u32[]{:S(2)}, u32[]{:S(2)}) collective-permute-start(f32[1024,3,1]{0,2,1:T(1,128)S(1)} %get-tuple-element.22), channel_id=1, source_target_pairs={{0,1},{1,2},{2,3},{3,4},{4,5},{5,6},{6,7},{7,8},{8,9},{9,10},{10,1... | collective-permute-start | bytes 36872 | tf_op jit(solution)/shard_map/ppermute | solution.py:27
  527.8 12.4 %collective-permute-start.23 = (f32[1024,3,1]{0,2,1:T(1,128)S(1)}, f32[1024,3,1]{0,2,1:T(1,128)S(1)}, u32[]{:S(2)}, u32[]{:S(2)}) collective-permute-start(f32[1024,3,1]{0,2,1:T(1,128)S(1)} %get-tuple-element.23), channel_id=1, source_target_pairs={{1,0},{2,1},{3,2},{4,3},{5,4},{6,5},{7,6},{8,7},{9,8},{10,9},{11,1... | collective-permute-start | bytes 36872 | tf_op jit(solution)/shard_map/ppermute | solution.py:29
  563.6 18.0 %all-to-all-start.5 = ((f32[1024,1,128]{2,1,0:T(1,128)}), f32[1024,1,128]{2,1,0:T(1,128)S(1)}, u32[]{:S(2)}, u32[]{:S(2)}) async-start(f32[1024,1,128]{2,1,0:T(1,128)} %bitcast.37), calls=%async_computation.5 | async-start | bytes 1048576 | tf_op jit(solution)/shard_map/all_to_all | solution.py:116
where the time goes:
time: 592 us; the launch traced here: 584 us
  other arithmetic  178 us (30%)
  starting transfers between devices  130 us (22%)
  waiting for transfers between devices  116 us (20%)
  matrix products  84.9 us (14%)
  local copies, waits for them, and re-layouts  55.1 us (9%)
  blocking collectives  17.9 us (3%)
    dot_general x4, matrix products, apply_table(): jnp.dot(matrix, flat, precision=lax.Precision.HIGHEST, preferred_element_...  84.9 us
    unnamed x5, other arithmetic  83.7 us
    ppermute x12, waiting for transfers between devices, extended(): lax.ppermute(tail, axis, [(i, (i + 1) % count) for i in range(ends)])  65 us
    reduce_sum x4, other arithmetic, per_device(): mref = jnp.mean(mobile_cols, axis=0, keepdims=True)  61 us
    ppermute x12, starting transfers between devices, extended(): lax.ppermute(head, axis, [((i + 1) % count, i) for i in range(ends)])  60.4 us
    ppermute x12, waiting for transfers between devices, extended(): lax.ppermute(head, axis, [((i + 1) % count, i) for i in range(ends)])  42.8 us
    unnamed x31, local copies, waits for them, and re-layouts  31.6 us
    ppermute x12, starting transfers between devices, extended(): lax.ppermute(tail, axis, [(i, (i + 1) % count) for i in range(ends)])  31.4 us
  transfers between devices with their start and end apart: 29, of which 17 were waited for; matrix products, arithmetic and copies ran while one was open for 33% of the time, Pallas kernels for 0%

commit v1 on v0

v1 whole, which is shorter than its diff:
```python
import math

import jax
import jax.numpy as jnp
from jax import lax
from jax.experimental import pallas as pl
from jax.experimental.pallas import tpu as pltpu
from jax.sharding import PartitionSpec as P

ND = 1024
CLASSES = 8
DEFECT = 2
SWEEPS = 3

STORE = 0.5
LOW = 0.05
HIGH = 1.95

LANES = 128
BLOCKS = 32
ROWS = ND // BLOCKS
GROUP = 16
AXES = ("cross", "strike")
FIELDS = 3
HALF = 2 * FIELDS


def chebyshev_weights(count):
    middle = 0.5 * (LOW + HIGH)
    half = 0.5 * (HIGH - LOW)
    return [
        1.0 / (middle + half * math.cos(math.pi * (2 * j + 1) / (2 * count))) for j in range(count)
    ]


def device_of(chunk):
    row, q = divmod(chunk, 8)
    return 64 * (row // 8) + 4 * (row % 8) + 32 * (q % 2) + q // 2


def exchange(vectors, keep=None):
    block = lax.broadcasted_iota(jnp.int32, vectors[0].shape, 1) // 8
    for step in (1, 8, 4, 2):
        high = (block & step) != 0
        done = []
        for b in range(GROUP):
            if step == 2 and keep is not None and b not in keep:
                done.append(None)
            elif b & step:
                other = pltpu.roll(vectors[b ^ step], LANES - 8 * step, 1)
                done.append(jnp.where(high, vectors[b], other))
            else:
                other = pltpu.roll(vectors[b ^ step], 8 * step, 1)
                done.append(jnp.where(high, other, vectors[b]))
        vectors = done
    return vectors


def pack_kernel(table, pressure, source, facies, out):
    def body(g, carry):
        tile, upper = g // 2, g % 2

        def read(ref):
            return [ref[pl.ds((upper * GROUP + b) * 32 + tile * 8, 8), :] for b in range(GROUP)]

        def lookup(codes):
            base = jnp.zeros(codes.shape, jnp.float32)
            for code in range(CLASSES):
                base = jnp.where(codes == code, table[code], base)
            return base

        fields = (read(pressure), [lookup(c) for c in read(facies)], read(source))
        for k, vectors in enumerate(fields):
            moved = exchange(vectors)
            for b in range(GROUP):
                first = 64 * tile + 32 * ((b >> 1) & 1) + (b >> 2)
                row = first * 2 * HALF + (b & 1) * HALF + k * 2 + upper
                out[pl.ds(row, 8, stride=8 * HALF), :] = moved[b]
        return carry

    lax.fori_loop(0, 8, body, 0)


def halves_kernel(recv, lower, upper):
    def body(g, carry):
        for w in range(HALF):
            rows = pl.ds(w * 256 + g * 8, 8)
            lower[rows, :] = recv[pl.ds(g * 8 * 2 * HALF + w, 8, stride=2 * HALF), :]
            upper[rows, :] = recv[pl.ds(g * 8 * 2 * HALF + HALF + w, 8, stride=2 * HALF), :]
        return carry

    lax.fori_loop(0, 32, body, 0)


def roll_lanes(x, shift):
    return pltpu.roll(x.reshape(64, LANES), shift % LANES, 1).reshape(x.shape)


def shift_blocks(x, shift):
    row = lax.broadcasted_iota(jnp.int32, (BLOCKS, LANES), 0)
    keep = (row >= shift) if shift > 0 else (row < BLOCKS + shift)
    parts = [
        jnp.where(keep, pltpu.roll(x[h].reshape(BLOCKS, LANES), shift % BLOCKS, 0), 0.0) for h in range(2)
    ]
    return jnp.stack(parts).reshape(x.shape)


def sides(x):
    lane = lax.broadcasted_iota(jnp.int32, (4, 8, LANES), 2)
    low, high = lane < 32, lane >= 96
    zero = jnp.zeros((4, 8, LANES), jnp.float32)
    r, l = roll_lanes(x, 32), roll_lanes(x, -32)
    left = jnp.stack([jnp.where(low, zero, r[0]), jnp.where(low, r[0], r[1])])
    right = jnp.stack([jnp.where(high, l[1], l[0]), jnp.where(high, zero, l[1])])
    return left, right, roll_lanes(x, 1), roll_lanes(x, -1)


def column_sum(x):
    total = jnp.sum(x, axis=(1, 2), keepdims=True)
    return jnp.broadcast_to(total, (2, 1, 8, LANES))


def work_kernel(own, left_halo, right_halo, out, p, m, base, source, resid, rho, part, power):
    omega = chebyshev_weights(SWEEPS)
    fields = (p, base, source)

    def unpack(g, carry):
        upper, h, tile = g // 8, (g // 4) % 2, g % 4
        for k in range(FIELDS):
            vectors = []
            w = k * 2 + upper
            for c in range(4):
                block = (4 * h + c) * 32 + tile * 8
                vectors.append(left_halo[pl.ds(w * 256 + block, 8), :])
                vectors.append(own[pl.ds(block * 2 * HALF + w, 8, stride=2 * HALF), :])
                vectors.append(own[pl.ds(block * 2 * HALF + HALF + w, 8, stride=2 * HALF), :])
                vectors.append(right_halo[pl.ds(w * 256 + block, 8), :])
            moved = exchange(vectors)
            for b in range(GROUP):
                fields[k][upper * GROUP + b + 1, h, tile] = moved[b]
        return carry

    lax.fori_loop(0, 16, unpack, 0)

    slab = (2, 4, 8, LANES)
    zero = jnp.zeros(slab, jnp.float32)

    def mobility(i, field):
        value = base[i + 1] * (1.0 + 0.5 * jnp.tanh(field))
        m[i + 1] = value
        return value

    total = lax.fori_loop(0, ROWS, lambda i, acc: acc + mobility(i, p[i + 1]), zero)

    for step in range(DEFECT):
        for ref in (p, m):
            ref[0] = shift_blocks(ref[ROWS], 1)
            ref[ROWS + 1] = shift_blocks(ref[1], -1)

        mref = column_sum(total) * (1.0 / ND)
        inside = mref > 0.0
        safe = jnp.where(inside, mref, 1.0)
        half = 0.5 * (4.0 + STORE / safe)
        ratio = 1.0 / (1.0 + half + jnp.sqrt(half * (half + 2.0)))
        gain = ratio / ((1.0 - ratio * ratio) * safe)

        def powers(i, value):
            value = value * ratio
            power[i] = value
            return value

        block_ratio = lax.fori_loop(0, ROWS, powers, jnp.ones((2, 1, 8, LANES), jnp.float32))
        squares = [block_ratio]
        for _ in range(5):
            squares.append(squares[-1] * squares[-1])
        whole = squares[5]
        reflect = 1.0 / (1.0 - whole * whole)
        index = lax.broadcasted_iota(jnp.int32, slab, 1) * 8 + lax.broadcasted_iota(jnp.int32, slab, 2)
        from_left = jnp.ones(slab, jnp.float32)
        from_right = jnp.ones(slab, jnp.float32)
        for bit in range(5):
            on = ((index >> bit) & 1) != 0
            from_left = jnp.where(on, from_left * squares[bit], from_left)
            from_right = jnp.where(on, from_right, from_right * squares[bit])

        def last(x, d):
            picked = jnp.where(index == d, x, 0.0)
            return column_sum(picked)

        def carries(ends, heads):
            for bit in range(5):
                ends = ends + squares[bit] * shift_blocks(ends, 1 << bit)
                heads = heads + squares[bit] * shift_blocks(heads, -(1 << bit))
            a, b = last(heads, 0), last(ends, BLOCKS - 1)
            before = shift_blocks(ends, 1) + from_left * ((a + whole * b) * reflect)
            after = shift_blocks(heads, -1) + from_right * ((b + whole * a) * reflect)
            return before, after

        def backward(values):
            def body(n, z):
                i = ROWS - 1 - n
                part[i] = part[i] + z
                return ratio * (values[i] + z)

            z = lax.fori_loop(0, ROWS - 1, body, zero, unroll=2)
            part[0] = part[0] + z
            return values[0] + z

        def form(i, y):
            here, mob = p[i + 1], m[i + 1]
            result = source[i + 1] - STORE * here
            near = [(p[i], m[i]), (p[i + 2], m[i + 2])] + list(zip(sides(here), sides(mob)))
            for other, other_m in near:
                result = result - 0.5 * (mob + other_m) * (here - other)
            result = jnp.where(inside, result, 0.0)
            resid[i] = result
            y = result + ratio * y
            part[i] = y
            return y

        ends = lax.fori_loop(0, ROWS, form, zero)
        values = resid
        for sweep in range(SWEEPS):
            before, after = carries(ends, backward(values))
            weight = omega[sweep]

            def solved(i):
                v = gain * (part[i] + power[i] * before + power[ROWS - 1 - i] * after)
                field = p[i + 1] + weight * v
                p[i + 1] = field
                return v, field

            if sweep + 1 < SWEEPS:
                previous, scaled = values, weight * mref

                def advance(i, y):
                    v, _ = solved(i)
                    a, b, c, d = sides(v)
                    value = (1.0 - weight) * previous[i] + scaled * (a + b + c + d)
                    rho[i] = value
                    y = value + ratio * y
                    part[i] = y
                    return y

                ends = lax.fori_loop(0, ROWS, advance, zero)
                values = rho
            elif step + 1 < DEFECT:
                total = lax.fori_loop(0, ROWS, lambda i, acc: acc + mobility(i, solved(i)[1]), zero)
            else:

                def finish(i, carry):
                    solved(i)
                    return carry

                lax.fori_loop(0, ROWS, finish, 0)

    kept = tuple(4 * c + s for c in range(4) for s in (1, 2))

    def pack(g, carry):
        upper, h, tile = g // 8, (g // 4) % 2, g % 4
        for k, (ref, offset) in enumerate(((p, 1), (resid, 0))):
            moved = exchange([ref[upper * GROUP + b + offset, h, tile] for b in range(GROUP)], kept)
            for c in range(4):
                block = (4 * h + c) * 32 + tile * 8
                for s in range(2):
                    row = block * 8 + s * 4 + k * 2 + upper
                    out[pl.ds(row, 8, stride=8), :] = moved[4 * c + 1 + s]
        return carry

    lax.fori_loop(0, 16, pack, 0)


def unpack_kernel(recv, pressure, defect):
    def body(g, carry):
        tile, upper = g // 2, g % 2
        for k, ref in enumerate((pressure, defect)):
            vectors = []
            for b in range(GROUP):
                first = 64 * tile + 32 * ((b >> 1) & 1) + (b >> 2)
                row = first * 8 + (b & 1) * 4 + k * 2 + upper
                vectors.append(recv[pl.ds(row, 8, stride=32), :])
            moved = exchange(vectors)
            for b in range(GROUP):
                ref[pl.ds((upper * GROUP + b) * 32 + tile * 8, 8), :] = moved[b]
        return carry

    lax.fori_loop(0, 8, body, 0)


def shape(rows):
    return jax.ShapeDtypeStruct((rows, LANES), jnp.float32)


VMEM = pl.BlockSpec(memory_space=pltpu.VMEM)
SMEM = pl.BlockSpec(memory_space=pltpu.SMEM)


def per_device(pressure, source, facies, mobility_table):
    flat = [x.reshape(ND, LANES) for x in (pressure, source, facies)]
    sent = pl.pallas_call(
        pack_kernel,
        out_shape=shape(3072),
        in_specs=[SMEM, VMEM, VMEM, VMEM],
        out_specs=VMEM,
        name="pack",
    )(mobility_table, *flat)
    recv = lax.all_to_all(sent.reshape(256, FIELDS, 4, LANES), AXES, 0, 0, tiled=True).reshape(3072, LANES)
    lower, upper = pl.pallas_call(
        halves_kernel,
        out_shape=(shape(1536), shape(1536)),
        in_specs=[VMEM],
        out_specs=(VMEM, VMEM),
        name="halves",
    )(recv)
    chain = [device_of(t) for t in range(256)]
    right_halo = lax.ppermute(lower, AXES, list(zip(chain[1:], chain[:-1])))
    left_halo = lax.ppermute(upper, AXES, list(zip(chain[:-1], chain[1:])))

    def cells(count):
        return pltpu.VMEM((count, 2, 4, 8, LANES), jnp.float32)

    result = pl.pallas_call(
        work_kernel,
        out_shape=shape(2048),
        in_specs=[VMEM, VMEM, VMEM],
        out_specs=VMEM,
        scratch_shapes=[
            cells(ROWS + 2),
            cells(ROWS + 2),
            cells(ROWS + 2),
            cells(ROWS + 2),
            cells(ROWS),
            cells(ROWS),
            cells(ROWS),
            pltpu.VMEM((ROWS, 2, 1, 8, LANES), jnp.float32),
        ],
        name="work",
    )(recv, left_halo, right_halo)
    back = lax.all_to_all(result.reshape(256, 8, LANES), AXES, 0, 0, tiled=True).reshape(2048, LANES)
    outs = pl.pallas_call(
        unpack_kernel,
        out_shape=(shape(ND), shape(ND)),
        in_specs=[VMEM],
        out_specs=(VMEM, VMEM),
        name="unpack",
    )(back)
    return tuple(x.reshape(pressure.shape) for x in outs)


def solution(mesh):
    spec = P("strike", "cross", None)
    return jax.shard_map(
        per_device,
        mesh=mesh,
        in_specs=(spec, spec, spec, P()),
        out_specs=(spec, spec),
        check_vma=False,
    )
```

time: 592 us -> 174 us (0.29)
  the two profiles are of different devices: /device:TPU:224 before, /device:TPU:1 now
where the time goes in v1:
time: 174 us; the launch traced here: 173 us
  blocking collectives  99.9 us (57%)
  Pallas kernels  54.1 us (31%)
  waiting for transfers between devices  11.6 us (7%)
  starting transfers between devices  6.24 us (4%)
    all_to_all x1, blocking collectives, per_device(): lax.all_to_all(sent.reshape(256, FIELDS, 4, LANES), AXES, 0, 0, tiled=True)  57.3 us
    all_to_all x1, blocking collectives, per_device(): lax.all_to_all(result.reshape(256, 8, LANES), AXES, 0, 0, tiled=True)  42.6 us
    pallas_call x1, Pallas kernels, per_device(): pl.pallas_call(work_kernel, out_shape=shape(2048), in_specs=[VMEM, VMEM,...  40.8 us
    ppermute x1, waiting for transfers between devices, per_device(): left_halo = lax.ppermute(upper, AXES, list(zip(chain[:-1], chain[1:])))  7.3 us
    pallas_call x1, Pallas kernels, per_device(): pl.pallas_call(pack_kernel, out_shape=shape(3072), in_specs=[SMEM, VMEM,...  5.48 us
    pallas_call x1, Pallas kernels, per_device(): pl.pallas_call(unpack_kernel, out_shape=(shape(ND), shape(ND)), in_specs=...  5.04 us
    ppermute x1, starting transfers between devices, per_device(): left_halo = lax.ppermute(upper, AXES, list(zip(chain[:-1], chain[1:])))  4.32 us
    ppermute x1, waiting for transfers between devices, per_device(): right_halo = lax.ppermute(lower, AXES, list(zip(chain[1:], chain[:-1])))  4.29 us
  transfers between devices with their start and end apart: 2, of which 2 were waited for; matrix products, arithmetic and copies ran while one was open for 0% of the time, Pallas kernels for 0%

profile of v1, /device:TPU:1, one launch (start us, length us, event | category | flops | bytes accessed | tf_op | source)
XLA Modules:
  0.0 173.4 jit_solution(14890057217336488631)
XLA Ops:
  0.6 5.5 %pack.1 = f32[3072,128]{1,0:T(8,128)} custom-call(f32[8]{0:T(128)} %table.1, f32[1024,128]{1,0:T(8,128)} %bitcast.14, f32[1024,128]{1,0:T(8,128)} %bitcast.15, s32[1024,128]{1,0:T(8,128)} %bitcast.16), custom_call_target="tpu_custom_call" | custom-call | tf_op jit(solution)/shard_map/pack/pallas_call | solution.py:300
  6.1 57.3 %all_to_all.10 = f32[256,3,4,128]{3,2,1,0:T(4,128)} all-to-all(f32[256,3,4,128]{3,2,1,0:T(4,128)} %bitcast.11), channel_id=1, replica_groups=mesh['cross'=8,'strike'=32] {'cross','strike'}, dimensions={0} | all-to-all | bytes 3145728 | tf_op jit(solution)/shard_map/all_to_all | solution.py:307
  63.4 2.8 %halves.1 = (f32[1536,128]{1,0:T(8,128)}, f32[1536,128]{1,0:T(8,128)}) custom-call(f32[3072,128]{1,0:T(8,128)} %bitcast.9), custom_call_target="tpu_custom_call" | custom-call | tf_op jit(solution)/shard_map/halves/pallas_call | solution.py:308
  66.2 4.3 %collective-permute-start = (f32[1536,128]{1,0:T(8,128)}, f32[1536,128]{1,0:T(8,128)S(1)}, u32[]{:S(2)}, u32[]{:S(2)}) collective-permute-start(f32[1536,128]{1,0:T(8,128)} %get-tuple-element.6), channel_id=1, source_target_pairs={{0,32},{32,1},{1,33},{33,2},{2,34},{34,3},{3,35},{35,4},{4,36},{36... | collective-permute-start | bytes 2359304 | tf_op jit(solution)/shard_map/ppermute | solution.py:317
  70.5 1.9 %collective-permute-start.1 = (f32[1536,128]{1,0:T(8,128)}, f32[1536,128]{1,0:T(8,128)S(1)}, u32[]{:S(2)}, u32[]{:S(2)}) collective-permute-start(f32[1536,128]{1,0:T(8,128)} %get-tuple-element.7), channel_id=1, source_target_pairs={{32,0},{1,32},{33,1},{2,33},{34,2},{3,34},{35,3},{4,35},{36,4},{5,... | collective-permute-start | bytes 2359304 | tf_op jit(solution)/shard_map/ppermute | solution.py:316
  72.5 7.3 %collective-permute-done.left_halo = f32[1536,128]{1,0:T(8,128)S(1)} collective-permute-done((f32[1536,128]{1,0:T(8,128)}, f32[1536,128]{1,0:T(8,128)S(1)}, u32[]{:S(2)}, u32[]{:S(2)}) %collective-permute-start) | collective-permute-done | bytes 786464 | tf_op jit(solution)/shard_map/ppermute | solution.py:317
  79.8 0.0 copy-start
  79.8 4.3 %collective-permute-done.1.right_halo = f32[1536,128]{1,0:T(8,128)S(1)} collective-permute-done((f32[1536,128]{1,0:T(8,128)}, f32[1536,128]{1,0:T(8,128)S(1)}, u32[]{:S(2)}, u32[]{:S(2)}) %collective-permute-start.1) | collective-permute-done | bytes 786464 | tf_op jit(solution)/shard_map/ppermute | solution.py:316
  84.0 0.0 copy-done
  84.0 0.0 copy-start.1
  84.1 0.9 copy-done.1
  84.9 40.8 %work.1 = f32[2048,128]{1,0:T(8,128)} custom-call(f32[3072,128]{1,0:T(8,128)} %bitcast.10, f32[1536,128]{1,0:T(8,128)} %copy-done, f32[1536,128]{1,0:T(8,128)} %copy-done.1), custom_call_target="tpu_custom_call" | custom-call | tf_op jit(solution)/shard_map/work/pallas_call | solution.py:322
  125.7 42.6 %all_to_all.11 = f32[256,8,128]{2,1,0:T(8,128)} all-to-all(f32[256,8,128]{2,1,0:T(8,128)} %bitcast.13), channel_id=1, replica_groups=mesh['cross'=8,'strike'=32] {'cross','strike'}, dimensions={0} | all-to-all | bytes 2097152 | tf_op jit(solution)/shard_map/all_to_all | solution.py:339
  168.3 5.0 %unpack.1 = (f32[1024,128]{1,0:T(8,128)}, f32[1024,128]{1,0:T(8,128)}) custom-call(f32[2048,128]{1,0:T(8,128)} %bitcast.12), custom_call_target="tpu_custom_call" | custom-call | tf_op jit(solution)/shard_map/unpack/pallas_call | solution.py:340
Async XLA Ops:
  66.2 13.6 %collective-permute-start = (f32[1536,128]{1,0:T(8,128)}, f32[1536,128]{1,0:T(8,128)S(1)}, u32[]{:S(2)}, u32[]{:S(2)}) collective-permute-start(f32[1536,128]{1,0:T(8,128)} %get-tuple-element.6), channel_id=1, source_target_pairs={{0,32},{32,1},{1,33},{33,2},{2,34},{34,3},{3,35},{35,4},{4,36},{36... | collective-permute-start | bytes 2359304 | tf_op jit(solution)/shard_map/ppermute | solution.py:317
  70.5 13.5 %collective-permute-start.1 = (f32[1536,128]{1,0:T(8,128)}, f32[1536,128]{1,0:T(8,128)S(1)}, u32[]{:S(2)}, u32[]{:S(2)}) collective-permute-start(f32[1536,128]{1,0:T(8,128)} %get-tuple-element.7), channel_id=1, source_target_pairs={{32,0},{1,32},{33,1},{2,33},{34,2},{3,34},{35,3},{4,35},{36,4},{5,... | collective-permute-start | bytes 2359304 | tf_op jit(solution)/shard_map/ppermute | solution.py:316
  79.8 4.3 %copy-start = (f32[1536,128]{1,0:T(8,128)}, f32[1536,128]{1,0:T(8,128)S(1)}, u32[]{:S(2)}) copy-start(f32[1536,128]{1,0:T(8,128)S(1)} %collective-permute-done.left_halo) | copy-start | bytes 2359300
  84.0 0.9 copy-start.1

commit v2 on v1

v2 whole, which is shorter than its diff:
```python
import math

import jax
import jax.numpy as jnp
from jax import lax
from jax.experimental import pallas as pl
from jax.experimental.pallas import tpu as pltpu
from jax.sharding import PartitionSpec as P

ND = 1024
CLASSES = 8
DEFECT = 2
SWEEPS = 3

STORE = 0.5
LOW = 0.05
HIGH = 1.95

LANES = 128
BLOCKS = 32
ROWS = ND // BLOCKS
GROUP = 16
AXES = ("cross", "strike")
FIELDS = 3
HALF = 2 * FIELDS


def chebyshev_weights(count):
    middle = 0.5 * (LOW + HIGH)
    half = 0.5 * (HIGH - LOW)
    return [
        1.0 / (middle + half * math.cos(math.pi * (2 * j + 1) / (2 * count))) for j in range(count)
    ]


def device_of(chunk):
    row, q = divmod(chunk, 8)
    z, s = divmod(row, 8)
    if s % 2:
        q = 7 - q
    place = s if s < 4 else 11 - s
    return 64 * z + 4 * place + 32 * (q % 2) + q // 2


def exchange(vectors, keep=range(GROUP)):
    block = lax.broadcasted_iota(jnp.int32, vectors[0].shape, 1) // 8
    vectors = [pltpu.roll(vectors[k], 8 * k, 1) if k else vectors[k] for k in range(GROUP)]
    vectors = [vectors[-k % GROUP] for k in range(GROUP)]
    for step in (1, 2, 4):
        here = (block & step) != 0
        vectors = [jnp.where(here, vectors[(k - step) % GROUP], vectors[k]) for k in range(GROUP)]
    here = block >= 8
    done = {}
    for b in keep:
        moved = jnp.where(here, vectors[(b - 8) % GROUP], vectors[b])
        done[b] = pltpu.roll(moved, LANES - 8 * b, 1) if b else moved
    return done


def snake_sublanes(vectors):
    row = lax.broadcasted_iota(jnp.int32, (8, LANES), 0)
    order = jnp.where(row < 4, row, 11 - row)
    return [jnp.take_along_axis(v, order, axis=0) for v in vectors]


def snake_chunks(vectors):
    row = lax.broadcasted_iota(jnp.int32, (8, LANES), 0)
    odd = ((row & 1) ^ (row >> 2)) != 0
    return [
        jnp.where(odd, vectors[GROUP - 2 - (k & -2) + (k & 1)], vectors[k]) for k in range(GROUP)
    ]


def pack_kernel(table, pressure, source, facies, out):
    def lookup(codes):
        base = jnp.zeros(codes.shape, jnp.float32)
        for code in range(CLASSES):
            base = jnp.where(codes == code, table[code], base)
        return base

    def body(upper, carry):
        def read(ref):
            return [ref[upper * GROUP + b] for b in range(GROUP)]

        fields = (read(pressure), [lookup(c) for c in read(facies)], read(source))
        for k, vectors in enumerate(fields):
            moved = snake_chunks(exchange(snake_sublanes(vectors)))
            for b in range(GROUP):
                row = (32 * ((b >> 1) & 1) + (b >> 2)) * 2 * HALF + (b & 1) * HALF + k * 2 + upper
                out[pl.ds(row, 8, stride=8 * HALF), :] = moved[b]
        return carry

    lax.fori_loop(0, 2, body, 0)


def halves_kernel(recv, lower, upper):
    def body(g, carry):
        for w in range(HALF):
            rows = pl.ds(w * 256 + g * 8, 8)
            lower[rows, :] = recv[pl.ds(g * 8 * 2 * HALF + w, 8, stride=2 * HALF), :]
            upper[rows, :] = recv[pl.ds(g * 8 * 2 * HALF + HALF + w, 8, stride=2 * HALF), :]
        return carry

    lax.fori_loop(0, 32, body, 0)


SLAB = (8, 8, LANES)


def roll_lanes(x, shift):
    return pltpu.roll(x.reshape(64, LANES), shift % LANES, 1).reshape(x.shape)


def shift_blocks(x, shift):
    lane = lax.broadcasted_iota(jnp.int32, SLAB, 2)
    if abs(shift) >= 8:
        lanes = shift * 4
        keep = (lane >= lanes) if shift > 0 else (lane < LANES + lanes)
        return jnp.where(keep, roll_lanes(x, lanes), 0.0)
    sub = lax.broadcasted_iota(jnp.int32, SLAB, 1)
    near = jnp.stack([pltpu.roll(x[c], shift % 8, 0) for c in range(8)])
    if shift > 0:
        far = jnp.where(lane >= 32, roll_lanes(near, 32), 0.0)
        return jnp.where(sub >= shift, near, far)
    far = jnp.where(lane < 96, roll_lanes(near, -32), 0.0)
    return jnp.where(sub < 8 + shift, near, far)


def column_sum(x):
    total = jnp.broadcast_to(jnp.sum(x, axis=1, keepdims=True), SLAB)
    total = total + roll_lanes(total, 32)
    return total + roll_lanes(total, 64)


def roll_sublanes(x, shift):
    return jnp.stack([pltpu.roll(x[c], shift % 8, 0) for c in range(8)])


def work_kernel(own, left_halo, right_halo, out, p, m, base, source, resid, rho, part, power):
    omega = chebyshev_weights(SWEEPS)
    fields = (p, base, source)

    def unpack(g, carry):
        upper, c = g // 8, g % 8
        for k in range(FIELDS):
            vectors = []
            w = k * 2 + upper
            for tile in range(4):
                block = c * 32 + tile * 8
                vectors.append(left_halo[pl.ds(w * 256 + block, 8), :])
                vectors.append(own[pl.ds(block * 2 * HALF + w, 8, stride=2 * HALF), :])
                vectors.append(own[pl.ds(block * 2 * HALF + HALF + w, 8, stride=2 * HALF), :])
                vectors.append(right_halo[pl.ds(w * 256 + block, 8), :])
            moved = exchange(vectors)
            for b in range(GROUP):
                fields[k][upper * GROUP + b + 1, c] = moved[b]
        return carry

    lax.fori_loop(0, 16, unpack, 0)

    zero = jnp.zeros(SLAB, jnp.float32)
    edge = jnp.zeros((1, 8, LANES), jnp.float32)
    lane = lax.broadcasted_iota(jnp.int32, SLAB, 2)
    sub = lax.broadcasted_iota(jnp.int32, SLAB, 1)

    def mobility(i, field):
        value = base[i + 1] * (1.0 + 0.5 * jnp.tanh(field))
        m[i + 1] = value
        return value

    total = lax.fori_loop(0, ROWS, lambda i, acc: acc + mobility(i, p[i + 1]), zero, unroll=2)

    for step in range(DEFECT):
        for ref in (p, m):
            ref[0] = shift_blocks(ref[ROWS], 1)
            ref[ROWS + 1] = shift_blocks(ref[1], -1)

        mref = column_sum(total) * (1.0 / ND)
        inside = mref > 0.0
        safe = jnp.where(inside, mref, 1.0)
        half = 0.5 * (4.0 + STORE / safe)
        ratio = 1.0 / (1.0 + half + jnp.sqrt(half * (half + 2.0)))
        gain = ratio / ((1.0 - ratio * ratio) * safe)
        inner = gain * mref
        gain = jnp.where(inside, gain, 0.0)

        def powers(i, value):
            power[i] = value
            return value * ratio

        block_ratio = lax.fori_loop(0, ROWS, powers, jnp.ones(SLAB, jnp.float32), unroll=2)
        power[ROWS] = block_ratio
        squares = [block_ratio]
        for _ in range(5):
            squares.append(squares[-1] * squares[-1])
        whole = squares[5]
        reflect = 1.0 / (1.0 - whole * whole)
        below_sub = jnp.ones(SLAB, jnp.float32)
        above_sub = jnp.ones(SLAB, jnp.float32)
        for bit in range(3):
            on = ((sub >> bit) & 1) != 0
            below_sub = jnp.where(on, below_sub * squares[bit], below_sub)
            above_sub = jnp.where(on, above_sub, above_sub * squares[bit])
        from_left, from_right = below_sub, above_sub
        for bit in range(2):
            on = ((lane >> (5 + bit)) & 1) != 0
            from_left = jnp.where(on, from_left * squares[3 + bit], from_left)
            from_right = jnp.where(on, from_right, from_right * squares[3 + bit])

        def spread(x, kept):
            x = jnp.where(kept, x, 0.0)
            x = x + roll_lanes(x, 32)
            return x + roll_lanes(x, 64)

        def carries(ends, heads):
            for bit in range(3):
                s = 1 << bit
                ends = ends + squares[bit] * jnp.where(sub >= s, roll_sublanes(ends, s), 0.0)
                heads = heads + squares[bit] * jnp.where(sub < 8 - s, roll_sublanes(heads, -s), 0.0)
            end = jnp.broadcast_to(ends[:, 7:8], SLAB)
            head = jnp.broadcast_to(heads[:, 0:1], SLAB)
            before, after = shift_blocks(end, 8), shift_blocks(head, -8)
            before = before + squares[3] * shift_blocks(before, 8)
            after = after + squares[3] * shift_blocks(after, -8)
            before = before + squares[4] * shift_blocks(before, 16)
            after = after + squares[4] * shift_blocks(after, -16)
            a = spread(head + squares[3] * after, lane < 32)
            b = spread(end + squares[3] * before, lane >= 96)
            before = jnp.where(sub > 0, roll_sublanes(ends, 1), 0.0) + below_sub * before
            after = jnp.where(sub < 7, roll_sublanes(heads, -1), 0.0) + above_sub * after
            before = before + from_left * ((a + whole * b) * reflect)
            after = after + from_right * ((b + whole * a) * reflect)
            return before, after

        def form(i, carry):
            y, other, above = carry
            here, mob = p[i + 1], m[i + 1]
            below = (mob + m[i + 2]) * (here - p[i + 2])
            flow = below - above
            wide, wide_m = jnp.concatenate([edge, here, edge]), jnp.concatenate([edge, mob, edge])
            across = (wide_m[:-1] + wide_m[1:]) * (wide[:-1] - wide[1:])
            flow = flow + (across[1:] - across[:-1])
            along = (mob + roll_lanes(mob, -1)) * (here - roll_lanes(here, -1))
            flow = flow + (along - roll_lanes(along, 1))
            result = source[i + 1] - STORE * here - 0.5 * flow
            if step + 1 == DEFECT:
                resid[i] = result
            value = gain * result
            rho[i] = value
            y = value + ratio * y
            part[i] = y
            return y, other + power[i] * value, below

        first = (m[0] + m[1]) * (p[0] - p[1])
        ends, heads, _ = lax.fori_loop(0, ROWS, form, (zero, zero, first), unroll=2)
        for sweep in range(SWEEPS):
            before, after = carries(ends, heads)
            down = sweep % 2 == 0
            entering, stored = (after, before) if down else (before, after)
            weight = omega[sweep]

            def solved(n, running):
                i = ROWS - 1 - n if down else n
                value = rho[i]
                opposite = ratio * running
                v = part[i] + power[ROWS - n] * stored + opposite
                field = p[i + 1] + weight * v
                p[i + 1] = field
                return i, value, value + opposite, v, field

            if sweep + 1 < SWEEPS:
                scaled = weight * inner

                def advance(n, carry):
                    running, x, other = carry
                    i, value, running, v, _ = solved(n, running)
                    near = roll_lanes(v, 1) + roll_lanes(v, -1)
                    near = near + (jnp.concatenate([edge, v[:-1]]) + jnp.concatenate([v[1:], edge]))
                    value = scaled * near if weight == 1.0 else (1.0 - weight) * value + scaled * near
                    rho[i] = value
                    x = value + ratio * x
                    part[i] = x
                    return running, x, other + power[n] * value

                _, x, other = lax.fori_loop(0, ROWS, advance, (entering, zero, zero), unroll=2)
                ends, heads = (other, x) if down else (x, other)
            elif step + 1 < DEFECT:

                def renew(n, carry):
                    running, acc = carry
                    i, _, running, _, field = solved(n, running)
                    return running, acc + mobility(i, field)

                total = lax.fori_loop(0, ROWS, renew, (entering, zero), unroll=2)[1]
            else:
                lax.fori_loop(0, ROWS, lambda n, running: solved(n, running)[2], entering, unroll=2)

    kept = tuple(4 * tile + s for tile in range(4) for s in (1, 2))

    def pack(g, carry):
        upper, c = g // 8, g % 8
        for k, (ref, offset) in enumerate(((p, 1), (resid, 0))):
            moved = exchange([ref[upper * GROUP + b + offset, c] for b in range(GROUP)], kept)
            for tile in range(4):
                for s in range(2):
                    row = (c * 32 + tile * 8) * 8 + s * 4 + k * 2 + upper
                    out[pl.ds(row, 8, stride=8), :] = moved[4 * tile + 1 + s]
        return carry

    lax.fori_loop(0, 16, pack, 0)


def unpack_kernel(recv, pressure, defect):
    def body(upper, carry):
        for k, ref in enumerate((pressure, defect)):
            vectors = []
            for b in range(GROUP):
                row = (32 * ((b >> 1) & 1) + (b >> 2)) * 8 + (b & 1) * 4 + k * 2 + upper
                vectors.append(recv[pl.ds(row, 8, stride=32), :])
            moved = exchange(snake_sublanes(snake_chunks(vectors)))
            for b in range(GROUP):
                ref[upper * GROUP + b] = moved[b]
        return carry

    lax.fori_loop(0, 2, body, 0)


def shape(rows):
    return jax.ShapeDtypeStruct((rows, LANES), jnp.float32)


VMEM = pl.BlockSpec(memory_space=pltpu.VMEM)
SMEM = pl.BlockSpec(memory_space=pltpu.SMEM)


def per_device(pressure, source, facies, mobility_table):
    flat = [x.reshape(ROWS, 32, LANES) for x in (pressure, source, facies)]
    tiles = pl.BlockSpec((ROWS, 8, LANES), lambda g: (0, g, 0))
    sent = pl.pallas_call(
        pack_kernel,
        out_shape=shape(3072),
        grid=(4,),
        in_specs=[SMEM, tiles, tiles, tiles],
        out_specs=pl.BlockSpec((768, LANES), lambda g: (g, 0)),
        name="pack",
    )(mobility_table, *flat)
    recv = lax.all_to_all(sent.reshape(256, FIELDS, 4, LANES), AXES, 0, 0, tiled=True).reshape(3072, LANES)
    lower, upper = pl.pallas_call(
        halves_kernel,
        out_shape=(shape(1536), shape(1536)),
        in_specs=[VMEM],
        out_specs=(VMEM, VMEM),
        name="halves",
    )(recv)
    chain = [device_of(t) for t in range(256)]
    right_halo = lax.ppermute(lower, AXES, list(zip(chain[1:], chain[:-1])))
    left_halo = lax.ppermute(upper, AXES, list(zip(chain[:-1], chain[1:])))

    def cells(count):
        return pltpu.VMEM((count,) + SLAB, jnp.float32)

    result = pl.pallas_call(
        work_kernel,
        out_shape=shape(2048),
        in_specs=[VMEM, VMEM, VMEM],
        out_specs=VMEM,
        scratch_shapes=[
            cells(ROWS + 2),
            cells(ROWS + 2),
            cells(ROWS + 2),
            cells(ROWS + 2),
            cells(ROWS),
            cells(ROWS),
            cells(ROWS),
            cells(ROWS + 1),
        ],
        name="work",
    )(recv, left_halo, right_halo)
    back = lax.all_to_all(result.reshape(256, 8, LANES), AXES, 0, 0, tiled=True).reshape(2048, LANES)
    outs = pl.pallas_call(
        unpack_kernel,
        out_shape=(jax.ShapeDtypeStruct((ROWS, 32, LANES), jnp.float32),) * 2,
        grid=(4,),
        in_specs=[pl.BlockSpec((512, LANES), lambda g: (g, 0))],
        out_specs=(tiles, tiles),
        name="unpack",
    )(back)
    return tuple(x.reshape(pressure.shape) for x in outs)


def solution(mesh):
    spec = P("strike", "cross", None)
    return jax.shard_map(
        per_device,
        mesh=mesh,
        in_specs=(spec, spec, spec, P()),
        out_specs=(spec, spec),
        check_vma=False,
    )
```

time: 174 us -> 154 us (0.89)
  Pallas kernels: 54.1 us -> 40.4 us
  blocking collectives: 99.9 us -> 93.6 us
    pallas_call x1, Pallas kernels: 40.8 us -> 28.8 us  [per_device(): pl.pallas_call(work_kernel, out_shape=shape(2048), in_specs=[VMEM, VMEM,...]
    all_to_all x1, blocking collectives: 42.6 us -> 36.3 us  [per_device(): lax.all_to_all(result.reshape(256, 8, LANES), AXES, 0, 0, tiled=True)]
where the time goes in v2:
time: 154 us; the launch traced here: 153 us
  blocking collectives  93.6 us (61%)
  Pallas kernels  40.4 us (26%)
  waiting for transfers between devices  11.6 us (8%)
  starting transfers between devices  6.24 us (4%)
    all_to_all x1, blocking collectives, per_device(): lax.all_to_all(sent.reshape(256, FIELDS, 4, LANES), AXES, 0, 0, tiled=True)  57.3 us
    all_to_all x1, blocking collectives, per_device(): lax.all_to_all(result.reshape(256, 8, LANES), AXES, 0, 0, tiled=True)  36.3 us
    pallas_call x1, Pallas kernels, per_device(): pl.pallas_call(work_kernel, out_shape=shape(2048), in_specs=[VMEM, VMEM,...  28.8 us
    ppermute x1, waiting for transfers between devices, per_device(): left_halo = lax.ppermute(upper, AXES, list(zip(chain[:-1], chain[1:])))  7.3 us
    pallas_call x1, Pallas kernels, per_device(): pl.pallas_call(pack_kernel, out_shape=shape(3072), grid=(4,), in_specs=[S...  4.55 us
    ppermute x1, starting transfers between devices, per_device(): left_halo = lax.ppermute(upper, AXES, list(zip(chain[:-1], chain[1:])))  4.32 us
    ppermute x1, waiting for transfers between devices, per_device(): right_halo = lax.ppermute(lower, AXES, list(zip(chain[1:], chain[:-1])))  4.29 us
    pallas_call x1, Pallas kernels, per_device(): pl.pallas_call(unpack_kernel, out_shape=(jax.ShapeDtypeStruct((ROWS, 32,...  4.25 us
  transfers between devices with their start and end apart: 2, of which 2 were waited for; matrix products, arithmetic and copies ran while one was open for 0% of the time, Pallas kernels for 0%

profile of v2, /device:TPU:1, one launch (start us, length us, event | category | flops | bytes accessed | tf_op | source)
XLA Modules:
  0.0 153.3 jit_solution(3086748323907684793)
XLA Ops:
  0.6 4.5 %pack.1 = f32[3072,128]{1,0:T(8,128)} custom-call(f32[8]{0:T(128)} %table.1, f32[32,32,128]{2,1,0:T(8,128)} %bitcast.14, f32[32,32,128]{2,1,0:T(8,128)} %bitcast.15, s32[32,32,128]{2,1,0:T(8,128)} %bitcast.16), custom_call_target="tpu_custom_call" | custom-call | tf_op jit(solution)/shard_map/pack/pallas_call | solution.py:339
  5.2 57.3 %all_to_all.10 = f32[256,3,4,128]{3,2,1,0:T(4,128)} all-to-all(f32[256,3,4,128]{3,2,1,0:T(4,128)} %bitcast.11), channel_id=1, replica_groups=mesh['cross'=8,'strike'=32] {'cross','strike'}, dimensions={0} | all-to-all | bytes 3145728 | tf_op jit(solution)/shard_map/all_to_all | solution.py:347
  62.5 2.8 %halves.1 = (f32[1536,128]{1,0:T(8,128)}, f32[1536,128]{1,0:T(8,128)}) custom-call(f32[3072,128]{1,0:T(8,128)} %bitcast.9), custom_call_target="tpu_custom_call" | custom-call | tf_op jit(solution)/shard_map/halves/pallas_call | solution.py:348
  65.3 4.3 %collective-permute-start = (f32[1536,128]{1,0:T(8,128)}, f32[1536,128]{1,0:T(8,128)S(1)}, u32[]{:S(2)}, u32[]{:S(2)}) collective-permute-start(f32[1536,128]{1,0:T(8,128)} %get-tuple-element.6), channel_id=1, source_target_pairs={{0,32},{32,1},{1,33},{33,2},{2,34},{34,3},{3,35},{35,39},{39,7},{7... | collective-permute-start | bytes 2359304 | tf_op jit(solution)/shard_map/ppermute | solution.py:357
  69.6 1.9 %collective-permute-start.1 = (f32[1536,128]{1,0:T(8,128)}, f32[1536,128]{1,0:T(8,128)S(1)}, u32[]{:S(2)}, u32[]{:S(2)}) collective-permute-start(f32[1536,128]{1,0:T(8,128)} %get-tuple-element.7), channel_id=1, source_target_pairs={{32,0},{1,32},{33,1},{2,33},{34,2},{3,34},{35,3},{39,35},{7,39},{3... | collective-permute-start | bytes 2359304 | tf_op jit(solution)/shard_map/ppermute | solution.py:356
  71.5 7.3 %collective-permute-done.left_halo = f32[1536,128]{1,0:T(8,128)S(1)} collective-permute-done((f32[1536,128]{1,0:T(8,128)}, f32[1536,128]{1,0:T(8,128)S(1)}, u32[]{:S(2)}, u32[]{:S(2)}) %collective-permute-start) | collective-permute-done | bytes 786464 | tf_op jit(solution)/shard_map/ppermute | solution.py:357
  78.8 0.0 copy-start
  78.8 4.3 %collective-permute-done.1.right_halo = f32[1536,128]{1,0:T(8,128)S(1)} collective-permute-done((f32[1536,128]{1,0:T(8,128)}, f32[1536,128]{1,0:T(8,128)S(1)}, u32[]{:S(2)}, u32[]{:S(2)}) %collective-permute-start.1) | collective-permute-done | bytes 786464 | tf_op jit(solution)/shard_map/ppermute | solution.py:356
  83.1 0.0 copy-done
  83.1 0.0 copy-start.1
  83.1 0.9 copy-done.1
  84.0 28.8 %work.1 = f32[2048,128]{1,0:T(8,128)} custom-call(f32[3072,128]{1,0:T(8,128)} %bitcast.10, f32[1536,128]{1,0:T(8,128)} %copy-done, f32[1536,128]{1,0:T(8,128)} %copy-done.1), custom_call_target="tpu_custom_call" | custom-call | tf_op jit(solution)/shard_map/work/pallas_call | solution.py:362
  112.8 36.3 %all_to_all.11 = f32[256,8,128]{2,1,0:T(8,128)} all-to-all(f32[256,8,128]{2,1,0:T(8,128)} %bitcast.13), channel_id=1, replica_groups=mesh['cross'=8,'strike'=32] {'cross','strike'}, dimensions={0} | all-to-all | bytes 2097152 | tf_op jit(solution)/shard_map/all_to_all | solution.py:379
  149.1 4.2 %unpack.1 = (f32[32,32,128]{2,1,0:T(8,128)}, f32[32,32,128]{2,1,0:T(8,128)}) custom-call(f32[2048,128]{1,0:T(8,128)} %bitcast.12), custom_call_target="tpu_custom_call" | custom-call | tf_op jit(solution)/shard_map/unpack/pallas_call | solution.py:380
Async XLA Ops:
  65.3 13.6 %collective-permute-start = (f32[1536,128]{1,0:T(8,128)}, f32[1536,128]{1,0:T(8,128)S(1)}, u32[]{:S(2)}, u32[]{:S(2)}) collective-permute-start(f32[1536,128]{1,0:T(8,128)} %get-tuple-element.6), channel_id=1, source_target_pairs={{0,32},{32,1},{1,33},{33,2},{2,34},{34,3},{3,35},{35,39},{39,7},{7... | collective-permute-start | bytes 2359304 | tf_op jit(solution)/shard_map/ppermute | solution.py:357
  69.6 13.5 %collective-permute-start.1 = (f32[1536,128]{1,0:T(8,128)}, f32[1536,128]{1,0:T(8,128)S(1)}, u32[]{:S(2)}, u32[]{:S(2)}) collective-permute-start(f32[1536,128]{1,0:T(8,128)} %get-tuple-element.7), channel_id=1, source_target_pairs={{32,0},{1,32},{33,1},{2,33},{34,2},{3,34},{35,3},{39,35},{7,39},{3... | collective-permute-start | bytes 2359304 | tf_op jit(solution)/shard_map/ppermute | solution.py:356
  78.8 4.3 %copy-start = (f32[1536,128]{1,0:T(8,128)}, f32[1536,128]{1,0:T(8,128)S(1)}, u32[]{:S(2)}) copy-start(f32[1536,128]{1,0:T(8,128)S(1)} %collective-permute-done.left_halo) | copy-start | bytes 2359300
  83.1 0.9 copy-start.1

commit v3 on v2

--- a/solution.py
+++ b/solution.py
@@ -22,6 +22,7 @@
 GROUP = 16
 AXES = ("cross", "strike")
 FIELDS = 3
+UNROLL = 4
 HALF = 2 * FIELDS
 
 
@@ -90,7 +91,7 @@
                 out[pl.ds(row, 8, stride=8 * HALF), :] = moved[b]
         return carry
 
-    lax.fori_loop(0, 2, body, 0)
+    lax.fori_loop(0, 2, body, 0, unroll=2)
 
 
 def halves_kernel(recv, lower, upper):
@@ -156,26 +157,29 @@
                 fields[k][upper * GROUP + b + 1, c] = moved[b]
         return carry
 
-    lax.fori_loop(0, 16, unpack, 0)
-
-    zero = jnp.zeros(SLAB, jnp.float32)
-    edge = jnp.zeros((1, 8, LANES), jnp.float32)
+    lax.fori_loop(0, 16, unpack, 0, unroll=2)
+
     lane = lax.broadcasted_iota(jnp.int32, SLAB, 2)
     sub = lax.broadcasted_iota(jnp.int32, SLAB, 1)
 
-    def mobility(i, field):
-        value = base[i + 1] * (1.0 + 0.5 * jnp.tanh(field))
-        m[i + 1] = value
+    zeros = tuple(jnp.zeros((8, LANES), jnp.float32) for _ in range(8))
+
+    def mobility(i, c, field):
+        value = base[i + 1, c] * (0.5 + 0.25 * jnp.tanh(field))
+        m[i + 1, c] = value
         return value
 
-    total = lax.fori_loop(0, ROWS, lambda i, acc: acc + mobility(i, p[i + 1]), zero, unroll=2)
+    def start(i, acc):
+        return tuple(acc[c] + mobility(i, c, p[i + 1, c]) for c in range(8))
+
+    total = jnp.stack(lax.fori_loop(0, ROWS, start, zeros, unroll=UNROLL))
 
     for step in range(DEFECT):
         for ref in (p, m):
             ref[0] = shift_blocks(ref[ROWS], 1)
             ref[ROWS + 1] = shift_blocks(ref[1], -1)
 
-        mref = column_sum(total) * (1.0 / ND)
+        mref = column_sum(total) * (2.0 / ND)
         inside = mref > 0.0
         safe = jnp.where(inside, mref, 1.0)
         half = 0.5 * (4.0 + STORE / safe)
@@ -232,68 +236,111 @@
             after = after + from_right * ((b + whole * a) * reflect)
             return before, after
 
+        first_gain = omega[0] * gain
+
+        def along(x, shift):
+            return pltpu.roll(x, shift % LANES, 1)
+
         def form(i, carry):
             y, other, above = carry
-            here, mob = p[i + 1], m[i + 1]
-            below = (mob + m[i + 2]) * (here - p[i + 2])
-            flow = below - above
-            wide, wide_m = jnp.concatenate([edge, here, edge]), jnp.concatenate([edge, mob, edge])
-            across = (wide_m[:-1] + wide_m[1:]) * (wide[:-1] - wide[1:])
-            flow = flow + (across[1:] - across[:-1])
-            along = (mob + roll_lanes(mob, -1)) * (here - roll_lanes(here, -1))
-            flow = flow + (along - roll_lanes(along, 1))
-            result = source[i + 1] - STORE * here - 0.5 * flow
-            if step + 1 == DEFECT:
-                resid[i] = result
-            value = gain * result
-            rho[i] = value
-            y = value + ratio * y
-            part[i] = y
-            return y, other + power[i] * value, below
-
-        first = (m[0] + m[1]) * (p[0] - p[1])
-        ends, heads, _ = lax.fori_loop(0, ROWS, form, (zero, zero, first), unroll=2)
+            here = [p[i + 1, c] for c in range(8)]
+            mob = [m[i + 1, c] for c in range(8)]
+            new_y, new_other, new_above = [], [], []
+            left = mob[0] * -here[0]
+            for c in range(8):
+                below = (mob[c] + m[i + 2, c]) * (here[c] - p[i + 2, c])
+                if c < 7:
+                    right = (mob[c] + mob[c + 1]) * (here[c] - here[c + 1])
+                else:
+                    right = mob[c] * here[c]
+                strike = (mob[c] + along(mob[c], -1)) * (here[c] - along(here[c], -1))
+                flow = (below - above[c]) + (right - left) + (strike - along(strike, 1))
+                left = right
+                result = (source[i + 1, c] - STORE * here[c]) - flow
+                if step + 1 == DEFECT:
+                    resid[i, c] = result
+                value = first_gain[c] * result
+                rho[i, c] = value
+                value_y = value + ratio[c] * y[c]
+                part[i, c] = value_y
+                new_y.append(value_y)
+                new_other.append(other[c] + power[i, c] * value)
+                new_above.append(below)
+            return tuple(new_y), tuple(new_other), tuple(new_above)
+
+        first = tuple((m[0, c] + m[1, c]) * (p[0, c] - p[1, c]) for c in range(8))
+        ends, heads, _ = lax.fori_loop(0, ROWS, form, (zeros, zeros, first), unroll=UNROLL)
         for sweep in range(SWEEPS):
-            before, after = carries(ends, heads)
+            before, after = carries(jnp.stack(ends), jnp.stack(heads))
             down = sweep % 2 == 0
             entering, stored = (after, before) if down else (before, after)
-            weight = omega[sweep]
-
-            def solved(n, running):
+            entering = tuple(entering[c] for c in range(8))
+
+            def solved(n, c, running):
                 i = ROWS - 1 - n if down else n
-                value = rho[i]
-                opposite = ratio * running
-                v = part[i] + power[ROWS - n] * stored + opposite
-                field = p[i + 1] + weight * v
-                p[i + 1] = field
-                return i, value, value + opposite, v, field
+                value = rho[i, c]
+                opposite = ratio[c] * running
+                v = (part[i, c] + opposite) + power[ROWS - n, c] * stored[c]
+                field = p[i + 1, c] + v
+                p[i + 1, c] = field
+                return value, value + opposite, v, field
 
             if sweep + 1 < SWEEPS:
-                scaled = weight * inner
+                scaled = omega[sweep + 1] * inner
+                keep = omega[sweep + 1] * (1.0 - omega[sweep]) / omega[sweep]
 
                 def advance(n, carry):
                     running, x, other = carry
-                    i, value, running, v, _ = solved(n, running)
-                    near = roll_lanes(v, 1) + roll_lanes(v, -1)
-                    near = near + (jnp.concatenate([edge, v[:-1]]) + jnp.concatenate([v[1:], edge]))
-                    value = scaled * near if weight == 1.0 else (1.0 - weight) * value + scaled * near
-                    rho[i] = value
-                    x = value + ratio * x
-                    part[i] = x
-                    return running, x, other + power[n] * value
-
-                _, x, other = lax.fori_loop(0, ROWS, advance, (entering, zero, zero), unroll=2)
+                    i = ROWS - 1 - n if down else n
+                    new_running, new_x, new_other = [], [], []
+                    values, vs = [], []
+
+                    def finish(c):
+                        near = along(vs[c], 1) + along(vs[c], -1)
+                        if c:
+                            near = near + vs[c - 1]
+                        if c < 7:
+                            near = near + vs[c + 1]
+                        value = scaled[c] * near
+                        if keep:
+                            value = keep * values[c] + value
+                        rho[i, c] = value
+                        value_x = value + ratio[c] * x[c]
+                        part[i, c] = value_x
+                        new_x.append(value_x)
+                        new_other.append(other[c] + power[n, c] * value)
+
+                    for c in range(8):
+                        value, run, v, _ = solved(n, c, running[c])
+                        values.append(value)
+                        new_running.append(run)
+                        vs.append(v)
+                        if c:
+                            finish(c - 1)
+                    finish(7)
+                    return tuple(new_running), tuple(new_x), tuple(new_other)
+
+                _, x, other = lax.fori_loop(0, ROWS, advance, (entering, zeros, zeros), unroll=UNROLL)
                 ends, heads = (other, x) if down else (x, other)
             elif step + 1 < DEFECT:
 
                 def renew(n, carry):
                     running, acc = carry
-                    i, _, running, _, field = solved(n, running)
-                    return running, acc + mobility(i, field)
-
-                total = lax.fori_loop(0, ROWS, renew, (entering, zero), unroll=2)[1]
+                    i = ROWS - 1 - n if down else n
+                    new_running, new_acc = [], []
+                    for c in range(8):
+                        _, run, _, field = solved(n, c, running[c])
+                        new_running.append(run)
+                        new_acc.append(acc[c] + mobility(i, c, field))
+                    return tuple(new_running), tuple(new_acc)
+
+                total = jnp.stack(lax.fori_loop(0, ROWS, renew, (entering, zeros), unroll=UNROLL)[1])
             else:
-                lax.fori_loop(0, ROWS, lambda n, running: solved(n, running)[2], entering, unroll=2)
+
+                def last(n, running):
+                    return tuple(solved(n, c, running[c])[1] for c in range(8))
+
+                lax.fori_loop(0, ROWS, last, entering, unroll=UNROLL)
 
     kept = tuple(4 * tile + s for tile in range(4) for s in (1, 2))
 
@@ -307,7 +354,7 @@
                     out[pl.ds(row, 8, stride=8), :] = moved[4 * tile + 1 + s]
         return carry
 
-    lax.fori_loop(0, 16, pack, 0)
+    lax.fori_loop(0, 16, pack, 0, unroll=2)
 
 
 def unpack_kernel(recv, pressure, defect):
@@ -322,7 +369,7 @@
                 ref[upper * GROUP + b] = moved[b]
         return carry
 
-    lax.fori_loop(0, 2, body, 0)
+    lax.fori_loop(0, 2, body, 0, unroll=2)
 
 
 def shape(rows):

time: 154 us -> 148 us (0.961)
  Pallas kernels: 40.4 us -> 34.8 us
    pallas_call x1, Pallas kernels: 28.8 us -> 23.6 us  [per_device(): pl.pallas_call(work_kernel, out_shape=shape(2048), in_specs=[VMEM, VMEM,...]
where the time goes in v3:
time: 148 us
  blocking collectives  93.6 us (63%)
  Pallas kernels  34.8 us (24%)
  waiting for transfers between devices  11.6 us (8%)
  starting transfers between devices  6.24 us (4%)
    all_to_all x1, blocking collectives, per_device(): lax.all_to_all(sent.reshape(256, FIELDS, 4, LANES), AXES, 0, 0, tiled=True)  57.3 us
    all_to_all x1, blocking collectives, per_device(): lax.all_to_all(result.reshape(256, 8, LANES), AXES, 0, 0, tiled=True)  36.3 us
    pallas_call x1, Pallas kernels, per_device(): pl.pallas_call(work_kernel, out_shape=shape(2048), in_specs=[VMEM, VMEM,...  23.6 us
    ppermute x1, waiting for transfers between devices, per_device(): left_halo = lax.ppermute(upper, AXES, list(zip(chain[:-1], chain[1:])))  7.3 us
    pallas_call x1, Pallas kernels, per_device(): pl.pallas_call(pack_kernel, out_shape=shape(3072), grid=(4,), in_specs=[S...  4.53 us
    ppermute x1, starting transfers between devices, per_device(): left_halo = lax.ppermute(upper, AXES, list(zip(chain[:-1], chain[1:])))  4.32 us
    ppermute x1, waiting for transfers between devices, per_device(): right_halo = lax.ppermute(lower, AXES, list(zip(chain[1:], chain[:-1])))  4.29 us
    pallas_call x1, Pallas kernels, per_device(): pl.pallas_call(unpack_kernel, out_shape=(jax.ShapeDtypeStruct((ROWS, 32,...  3.88 us
  transfers between devices with their start and end apart: 2, of which 2 were waited for; matrix products, arithmetic and copies ran while one was open for 0% of the time, Pallas kernels for 0%

profile of v3, /device:TPU:1, one launch (start us, length us, event | category | flops | bytes accessed | tf_op | source)
XLA Modules:
  0.0 147.8 jit_solution(3701313364770428974)
XLA Ops:
  0.6 4.5 %pack.1 = f32[3072,128]{1,0:T(8,128)} custom-call(f32[8]{0:T(128)} %table.1, f32[32,32,128]{2,1,0:T(8,128)} %bitcast.14, f32[32,32,128]{2,1,0:T(8,128)} %bitcast.15, s32[32,32,128]{2,1,0:T(8,128)} %bitcast.16), custom_call_target="tpu_custom_call" | custom-call | tf_op jit(solution)/shard_map/pack/pallas_call | solution.py:386
  5.2 57.3 %all_to_all.10 = f32[256,3,4,128]{3,2,1,0:T(4,128)} all-to-all(f32[256,3,4,128]{3,2,1,0:T(4,128)} %bitcast.11), channel_id=1, replica_groups=mesh['cross'=8,'strike'=32] {'cross','strike'}, dimensions={0} | all-to-all | bytes 3145728 | tf_op jit(solution)/shard_map/all_to_all | solution.py:394
  62.5 2.8 %halves.1 = (f32[1536,128]{1,0:T(8,128)}, f32[1536,128]{1,0:T(8,128)}) custom-call(f32[3072,128]{1,0:T(8,128)} %bitcast.9), custom_call_target="tpu_custom_call" | custom-call | tf_op jit(solution)/shard_map/halves/pallas_call | solution.py:395
  65.3 4.3 %collective-permute-start = (f32[1536,128]{1,0:T(8,128)}, f32[1536,128]{1,0:T(8,128)S(1)}, u32[]{:S(2)}, u32[]{:S(2)}) collective-permute-start(f32[1536,128]{1,0:T(8,128)} %get-tuple-element.6), channel_id=1, source_target_pairs={{0,32},{32,1},{1,33},{33,2},{2,34},{34,3},{3,35},{35,39},{39,7},{7... | collective-permute-start | bytes 2359304 | tf_op jit(solution)/shard_map/ppermute | solution.py:404
  69.6 1.9 %collective-permute-start.1 = (f32[1536,128]{1,0:T(8,128)}, f32[1536,128]{1,0:T(8,128)S(1)}, u32[]{:S(2)}, u32[]{:S(2)}) collective-permute-start(f32[1536,128]{1,0:T(8,128)} %get-tuple-element.7), channel_id=1, source_target_pairs={{32,0},{1,32},{33,1},{2,33},{34,2},{3,34},{35,3},{39,35},{7,39},{3... | collective-permute-start | bytes 2359304 | tf_op jit(solution)/shard_map/ppermute | solution.py:403
  71.5 7.3 %collective-permute-done.left_halo = f32[1536,128]{1,0:T(8,128)S(1)} collective-permute-done((f32[1536,128]{1,0:T(8,128)}, f32[1536,128]{1,0:T(8,128)S(1)}, u32[]{:S(2)}, u32[]{:S(2)}) %collective-permute-start) | collective-permute-done | bytes 786464 | tf_op jit(solution)/shard_map/ppermute | solution.py:404
  78.8 0.0 copy-start
  78.8 4.3 %collective-permute-done.1.right_halo = f32[1536,128]{1,0:T(8,128)S(1)} collective-permute-done((f32[1536,128]{1,0:T(8,128)}, f32[1536,128]{1,0:T(8,128)S(1)}, u32[]{:S(2)}, u32[]{:S(2)}) %collective-permute-start.1) | collective-permute-done | bytes 786464 | tf_op jit(solution)/shard_map/ppermute | solution.py:403
  83.1 0.0 copy-done
  83.1 0.0 copy-start.1
  83.1 0.9 copy-done.1
  84.0 23.6 %work.1 = f32[2048,128]{1,0:T(8,128)} custom-call(f32[3072,128]{1,0:T(8,128)} %bitcast.10, f32[1536,128]{1,0:T(8,128)} %copy-done, f32[1536,128]{1,0:T(8,128)} %copy-done.1), custom_call_target="tpu_custom_call" | custom-call | tf_op jit(solution)/shard_map/work/pallas_call | solution.py:409
  107.6 36.3 %all_to_all.11 = f32[256,8,128]{2,1,0:T(8,128)} all-to-all(f32[256,8,128]{2,1,0:T(8,128)} %bitcast.13), channel_id=1, replica_groups=mesh['cross'=8,'strike'=32] {'cross','strike'}, dimensions={0} | all-to-all | bytes 2097152 | tf_op jit(solution)/shard_map/all_to_all | solution.py:426
  143.9 3.9 %unpack.1 = (f32[32,32,128]{2,1,0:T(8,128)}, f32[32,32,128]{2,1,0:T(8,128)}) custom-call(f32[2048,128]{1,0:T(8,128)} %bitcast.12), custom_call_target="tpu_custom_call" | custom-call | tf_op jit(solution)/shard_map/unpack/pallas_call | solution.py:427
Async XLA Ops:
  65.3 13.6 %collective-permute-start = (f32[1536,128]{1,0:T(8,128)}, f32[1536,128]{1,0:T(8,128)S(1)}, u32[]{:S(2)}, u32[]{:S(2)}) collective-permute-start(f32[1536,128]{1,0:T(8,128)} %get-tuple-element.6), channel_id=1, source_target_pairs={{0,32},{32,1},{1,33},{33,2},{2,34},{34,3},{3,35},{35,39},{39,7},{7... | collective-permute-start | bytes 2359304 | tf_op jit(solution)/shard_map/ppermute | solution.py:404
  69.6 13.5 %collective-permute-start.1 = (f32[1536,128]{1,0:T(8,128)}, f32[1536,128]{1,0:T(8,128)S(1)}, u32[]{:S(2)}, u32[]{:S(2)}) collective-permute-start(f32[1536,128]{1,0:T(8,128)} %get-tuple-element.7), channel_id=1, source_target_pairs={{32,0},{1,32},{33,1},{2,33},{34,2},{3,34},{35,3},{39,35},{7,39},{3... | collective-permute-start | bytes 2359304 | tf_op jit(solution)/shard_map/ppermute | solution.py:403
  78.8 4.3 %copy-start = (f32[1536,128]{1,0:T(8,128)}, f32[1536,128]{1,0:T(8,128)S(1)}, u32[]{:S(2)}) copy-start(f32[1536,128]{1,0:T(8,128)S(1)} %collective-permute-done.left_halo) | copy-start | bytes 2359300
  83.1 0.9 copy-start.1

commit v4 on v3

--- a/solution.py
+++ b/solution.py
@@ -94,15 +94,56 @@
     lax.fori_loop(0, 2, body, 0, unroll=2)
 
 
-def halves_kernel(recv, lower, upper):
-    def body(g, carry):
-        for w in range(HALF):
-            rows = pl.ds(w * 256 + g * 8, 8)
-            lower[rows, :] = recv[pl.ds(g * 8 * 2 * HALF + w, 8, stride=2 * HALF), :]
-            upper[rows, :] = recv[pl.ds(g * 8 * 2 * HALF + HALF + w, 8, stride=2 * HALF), :]
+def cell_index():
+    return lax.broadcasted_iota(jnp.int32, (8, LANES), 1) % 8
+
+
+def squeeze(four, tail):
+    cell = cell_index()
+    free = cell < 2 if tail else cell >= 6
+    sign = -1 if tail else 1
+    shifts = (2, 4, 6) if tail else (6, 4, 2)
+    return [jnp.where(free, pltpu.roll(four[3], sign * n % LANES, 1), v) for v, n in zip(four, shifts)]
+
+
+def stretch(three, tail):
+    cell = cell_index()
+    if tail:
+        a, b, c = (pltpu.roll(v, n, 1) for v, n in zip(three, (2, 4, 6)))
+        return list(three) + [jnp.where(cell >= 6, c, jnp.where(cell >= 4, b, a))]
+    a, b, c = (pltpu.roll(v, LANES - n, 1) for v, n in zip(three, (6, 4, 2)))
+    return list(three) + [jnp.where(cell < 2, a, jnp.where(cell < 4, b, c))]
+
+
+def halves_kernel(recv, lower, upper, whole, first, second, sems):
+    def arrival(c):
+        span = pl.ds(c * 64 * HALF, 64 * HALF)
+        return pltpu.make_async_copy(recv.at[span], whole.at[span], sems.at[2, c])
+
+    def departure(c, side):
+        span = pl.ds(c * 24 * HALF, 24 * HALF)
+        return pltpu.make_async_copy((first, second)[side].at[span], (lower, upper)[side].at[span], sems.at[side, c])
+
+    for c in range(8):
+        arrival(c).start()
+
+    def body(c, carry):
+        arrival(c).wait()
+        for side, ref in enumerate((first, second)):
+            for w in range(HALF):
+                four = [
+                    whole[pl.ds((c * 32 + tile * 8) * 2 * HALF + side * HALF + w, 8, stride=2 * HALF), :]
+                    for tile in range(4)
+                ]
+                for n, vector in enumerate(squeeze(four, side == 1)):
+                    ref[pl.ds((c * HALF + w) * 24 + n * 8, 8), :] = vector
+            departure(c, side).start()
         return carry
 
-    lax.fori_loop(0, 32, body, 0)
+    lax.fori_loop(0, 8, body, 0)
+    for c in range(8):
+        for side in range(2):
+            departure(c, side).wait()
 
 
 SLAB = (8, 8, LANES)
@@ -137,27 +178,45 @@
     return jnp.stack([pltpu.roll(x[c], shift % 8, 0) for c in range(8)])
 
 
-def work_kernel(own, left_halo, right_halo, out, p, m, base, source, resid, rho, part, power):
+def work_kernel(
+    own_in, left_in, right_in, out, p, m, base, source, resid, rho, part, power, own, left, right, sent, sems
+):
     omega = chebyshev_weights(SWEEPS)
     fields = (p, base, source)
 
-    def unpack(g, carry):
-        upper, c = g // 8, g % 8
-        for k in range(FIELDS):
-            vectors = []
-            w = k * 2 + upper
-            for tile in range(4):
-                block = c * 32 + tile * 8
-                vectors.append(left_halo[pl.ds(w * 256 + block, 8), :])
-                vectors.append(own[pl.ds(block * 2 * HALF + w, 8, stride=2 * HALF), :])
-                vectors.append(own[pl.ds(block * 2 * HALF + HALF + w, 8, stride=2 * HALF), :])
-                vectors.append(right_halo[pl.ds(w * 256 + block, 8), :])
-            moved = exchange(vectors)
-            for b in range(GROUP):
-                fields[k][upper * GROUP + b + 1, c] = moved[b]
+    def arrivals(c):
+        for k, (there, here, rows) in enumerate(
+            ((own_in, own, 64 * HALF), (left_in, left, 24 * HALF), (right_in, right, 24 * HALF))
+        ):
+            span = pl.ds(c * rows, rows)
+            yield pltpu.make_async_copy(there.at[span], here.at[span], sems.at[k, c])
+
+    for c in range(8):
+        for copy in arrivals(c):
+            copy.start()
+
+    def unpack(c, carry):
+        for copy in arrivals(c):
+            copy.wait()
+        for upper in range(2):
+            for k in range(FIELDS):
+                vectors = []
+                w = k * 2 + upper
+                first = (c * HALF + w) * 24
+                before = stretch([left[pl.ds(first + n * 8, 8), :] for n in range(3)], True)
+                after = stretch([right[pl.ds(first + n * 8, 8), :] for n in range(3)], False)
+                for tile in range(4):
+                    block = c * 32 + tile * 8
+                    vectors.append(before[tile])
+                    vectors.append(own[pl.ds(block * 2 * HALF + w, 8, stride=2 * HALF), :])
+                    vectors.append(own[pl.ds(block * 2 * HALF + HALF + w, 8, stride=2 * HALF), :])
+                    vectors.append(after[tile])
+                moved = exchange(vectors)
+                for b in range(GROUP):
+                    fields[k][upper * GROUP + b + 1, c] = moved[b]
         return carry
 
-    lax.fori_loop(0, 16, unpack, 0, unroll=2)
+    lax.fori_loop(0, 8, unpack, 0)
 
     lane = lax.broadcasted_iota(jnp.int32, SLAB, 2)
     sub = lax.broadcasted_iota(jnp.int32, SLAB, 1)
@@ -344,17 +403,24 @@
 
     kept = tuple(4 * tile + s for tile in range(4) for s in (1, 2))
 
-    def pack(g, carry):
-        upper, c = g // 8, g % 8
-        for k, (ref, offset) in enumerate(((p, 1), (resid, 0))):
-            moved = exchange([ref[upper * GROUP + b + offset, c] for b in range(GROUP)], kept)
-            for tile in range(4):
-                for s in range(2):
-                    row = (c * 32 + tile * 8) * 8 + s * 4 + k * 2 + upper
-                    out[pl.ds(row, 8, stride=8), :] = moved[4 * tile + 1 + s]
+    def departure(c):
+        span = pl.ds(c * 256, 256)
+        return pltpu.make_async_copy(sent.at[span], out.at[span], sems.at[3, c])
+
+    def pack(c, carry):
+        for upper in range(2):
+            for k, (ref, offset) in enumerate(((p, 1), (resid, 0))):
+                moved = exchange([ref[upper * GROUP + b + offset, c] for b in range(GROUP)], kept)
+                for tile in range(4):
+                    for s in range(2):
+                        row = (c * 32 + tile * 8) * 8 + s * 4 + k * 2 + upper
+                        sent[pl.ds(row, 8, stride=8), :] = moved[4 * tile + 1 + s]
+        departure(c).start()
         return carry
 
-    lax.fori_loop(0, 16, pack, 0, unroll=2)
+    lax.fori_loop(0, 8, pack, 0)
+    for c in range(8):
+        departure(c).wait()
 
 
 def unpack_kernel(recv, pressure, defect):
@@ -376,6 +442,7 @@
     return jax.ShapeDtypeStruct((rows, LANES), jnp.float32)
 
 
+ANY = pl.BlockSpec(memory_space=pl.ANY)
 VMEM = pl.BlockSpec(memory_space=pltpu.VMEM)
 SMEM = pl.BlockSpec(memory_space=pltpu.SMEM)
 
@@ -394,9 +461,15 @@
     recv = lax.all_to_all(sent.reshape(256, FIELDS, 4, LANES), AXES, 0, 0, tiled=True).reshape(3072, LANES)
     lower, upper = pl.pallas_call(
         halves_kernel,
-        out_shape=(shape(1536), shape(1536)),
-        in_specs=[VMEM],
-        out_specs=(VMEM, VMEM),
+        out_shape=(shape(1152), shape(1152)),
+        in_specs=[ANY],
+        out_specs=(ANY, ANY),
+        scratch_shapes=[
+            pltpu.VMEM((3072, LANES), jnp.float32),
+            pltpu.VMEM((1152, LANES), jnp.float32),
+            pltpu.VMEM((1152, LANES), jnp.float32),
+            pltpu.SemaphoreType.DMA((3, 8)),
+        ],
         name="halves",
     )(recv)
     chain = [device_of(t) for t in range(256)]
@@ -409,8 +482,8 @@
     result = pl.pallas_call(
         work_kernel,
         out_shape=shape(2048),
-        in_specs=[VMEM, VMEM, VMEM],
-        out_specs=VMEM,
+        in_specs=[ANY, ANY, ANY],
+        out_specs=ANY,
         scratch_shapes=[
             cells(ROWS + 2),
             cells(ROWS + 2),
@@ -420,6 +493,11 @@
             cells(ROWS),
             cells(ROWS),
             cells(ROWS + 1),
+            pltpu.VMEM((3072, LANES), jnp.float32),
+            pltpu.VMEM((1152, LANES), jnp.float32),
+            pltpu.VMEM((1152, LANES), jnp.float32),
+            pltpu.VMEM((2048, LANES), jnp.float32),
+            pltpu.SemaphoreType.DMA((4, 8)),
         ],
         name="work",
     )(recv, left_halo, right_halo)

time: 148 us -> 145 us (0.980)
  waiting for transfers between devices: 11.6 us -> 9.48 us
    ppermute x1, waiting for transfers between devices: 7.3 us -> 5.19 us  [per_device(): left_halo = lax.ppermute(upper, AXES, list(zip(chain[:-1], chain[1:])))]
where the time goes in v4:
time: 145 us
  blocking collectives  93.6 us (65%)
  Pallas kernels  34.2 us (24%)
  waiting for transfers between devices  9.48 us (7%)
  starting transfers between devices  6.25 us (4%)
    all_to_all x1, blocking collectives, per_device(): lax.all_to_all(sent.reshape(256, FIELDS, 4, LANES), AXES, 0, 0, tiled=True)  57.3 us
    all_to_all x1, blocking collectives, per_device(): lax.all_to_all(result.reshape(256, 8, LANES), AXES, 0, 0, tiled=True)  36.3 us
    pallas_call x1, Pallas kernels, per_device(): pl.pallas_call(work_kernel, out_shape=shape(2048), in_specs=[ANY, ANY, AN...  23.2 us
    ppermute x1, waiting for transfers between devices, per_device(): left_halo = lax.ppermute(upper, AXES, list(zip(chain[:-1], chain[1:])))  5.19 us
    pallas_call x1, Pallas kernels, per_device(): pl.pallas_call(pack_kernel, out_shape=shape(3072), grid=(4,), in_specs=[S...  4.53 us
    ppermute x1, starting transfers between devices, per_device(): left_halo = lax.ppermute(upper, AXES, list(zip(chain[:-1], chain[1:])))  4.33 us
    ppermute x1, waiting for transfers between devices, per_device(): right_halo = lax.ppermute(lower, AXES, list(zip(chain[1:], chain[:-1])))  4.29 us
    pallas_call x1, Pallas kernels, per_device(): pl.pallas_call(unpack_kernel, out_shape=(jax.ShapeDtypeStruct((ROWS, 32,...  3.88 us
  transfers between devices with their start and end apart: 2, of which 2 were waited for; matrix products, arithmetic and copies ran while one was open for 0% of the time, Pallas kernels for 0%

profile of v4, /device:TPU:1, one launch (start us, length us, event | category | flops | bytes accessed | tf_op | source)
XLA Modules:
  0.0 145.0 jit_solution(4489288277228003794)
XLA Ops:
  0.6 4.5 %pack.1 = f32[3072,128]{1,0:T(8,128)} custom-call(f32[8]{0:T(128)} %table.1, f32[32,32,128]{2,1,0:T(8,128)} %bitcast.14, f32[32,32,128]{2,1,0:T(8,128)} %bitcast.15, s32[32,32,128]{2,1,0:T(8,128)} %bitcast.16), custom_call_target="tpu_custom_call" | custom-call | tf_op jit(solution)/shard_map/pack/pallas_call | solution.py:453
  5.2 57.3 %all_to_all.10 = f32[256,3,4,128]{3,2,1,0:T(4,128)} all-to-all(f32[256,3,4,128]{3,2,1,0:T(4,128)} %bitcast.11), channel_id=1, replica_groups=mesh['cross'=8,'strike'=32] {'cross','strike'}, dimensions={0} | all-to-all | bytes 3145728 | tf_op jit(solution)/shard_map/all_to_all | solution.py:461
  62.5 2.6 %halves.1 = (f32[1152,128]{1,0:T(8,128)}, f32[1152,128]{1,0:T(8,128)}) custom-call(f32[3072,128]{1,0:T(8,128)} %bitcast.9), custom_call_target="tpu_custom_call" | custom-call | tf_op jit(solution)/shard_map/halves/pallas_call | solution.py:462
  65.1 4.3 %collective-permute-start = (f32[1152,128]{1,0:T(8,128)}, f32[1152,128]{1,0:T(8,128)S(1)}, u32[]{:S(2)}, u32[]{:S(2)}) collective-permute-start(f32[1152,128]{1,0:T(8,128)} %get-tuple-element.6), channel_id=1, source_target_pairs={{0,32},{32,1},{1,33},{33,2},{2,34},{34,3},{3,35},{35,39},{39,7},{7... | collective-permute-start | bytes 1769480 | tf_op jit(solution)/shard_map/ppermute | solution.py:477
  69.4 1.9 %collective-permute-start.1 = (f32[1152,128]{1,0:T(8,128)}, f32[1152,128]{1,0:T(8,128)S(1)}, u32[]{:S(2)}, u32[]{:S(2)}) collective-permute-start(f32[1152,128]{1,0:T(8,128)} %get-tuple-element.7), channel_id=1, source_target_pairs={{32,0},{1,32},{33,1},{2,33},{34,2},{3,34},{35,3},{39,35},{7,39},{3... | collective-permute-start | bytes 1769480 | tf_op jit(solution)/shard_map/ppermute | solution.py:476
  71.4 5.2 %collective-permute-done.left_in = f32[1152,128]{1,0:T(8,128)S(1)} collective-permute-done((f32[1152,128]{1,0:T(8,128)}, f32[1152,128]{1,0:T(8,128)S(1)}, u32[]{:S(2)}, u32[]{:S(2)}) %collective-permute-start) | collective-permute-done | bytes 589856 | tf_op jit(solution)/shard_map/ppermute | solution.py:477
  76.6 0.0 copy-start
  76.6 4.3 %collective-permute-done.1.right_in = f32[1152,128]{1,0:T(8,128)S(1)} collective-permute-done((f32[1152,128]{1,0:T(8,128)}, f32[1152,128]{1,0:T(8,128)S(1)}, u32[]{:S(2)}, u32[]{:S(2)}) %collective-permute-start.1) | collective-permute-done | bytes 589856 | tf_op jit(solution)/shard_map/ppermute | solution.py:476
  80.9 0.0 copy-done
  80.9 0.0 copy-start.1
  80.9 0.8 copy-done.1
  81.7 23.2 %work.1 = f32[2048,128]{1,0:T(8,128)} custom-call(f32[3072,128]{1,0:T(8,128)} %bitcast.10, f32[1152,128]{1,0:T(8,128)} %copy-done, f32[1152,128]{1,0:T(8,128)} %copy-done.1), custom_call_target="tpu_custom_call" | custom-call | tf_op jit(solution)/shard_map/work/pallas_call | solution.py:482
  104.9 36.3 %all_to_all.11 = f32[256,8,128]{2,1,0:T(8,128)} all-to-all(f32[256,8,128]{2,1,0:T(8,128)} %bitcast.13), channel_id=1, replica_groups=mesh['cross'=8,'strike'=32] {'cross','strike'}, dimensions={0} | all-to-all | bytes 2097152 | tf_op jit(solution)/shard_map/all_to_all | solution.py:504
  141.2 3.9 %unpack.1 = (f32[32,32,128]{2,1,0:T(8,128)}, f32[32,32,128]{2,1,0:T(8,128)}) custom-call(f32[2048,128]{1,0:T(8,128)} %bitcast.12), custom_call_target="tpu_custom_call" | custom-call | tf_op jit(solution)/shard_map/unpack/pallas_call | solution.py:505
Async XLA Ops:
  65.1 11.5 %collective-permute-start = (f32[1152,128]{1,0:T(8,128)}, f32[1152,128]{1,0:T(8,128)S(1)}, u32[]{:S(2)}, u32[]{:S(2)}) collective-permute-start(f32[1152,128]{1,0:T(8,128)} %get-tuple-element.6), channel_id=1, source_target_pairs={{0,32},{32,1},{1,33},{33,2},{2,34},{34,3},{3,35},{35,39},{39,7},{7... | collective-permute-start | bytes 1769480 | tf_op jit(solution)/shard_map/ppermute | solution.py:477
  69.4 11.4 %collective-permute-start.1 = (f32[1152,128]{1,0:T(8,128)}, f32[1152,128]{1,0:T(8,128)S(1)}, u32[]{:S(2)}, u32[]{:S(2)}) collective-permute-start(f32[1152,128]{1,0:T(8,128)} %get-tuple-element.7), channel_id=1, source_target_pairs={{32,0},{1,32},{33,1},{2,33},{34,2},{3,34},{35,3},{39,35},{7,39},{3... | collective-permute-start | bytes 1769480 | tf_op jit(solution)/shard_map/ppermute | solution.py:476
  76.6 4.3 %copy-start = (f32[1152,128]{1,0:T(8,128)}, f32[1152,128]{1,0:T(8,128)S(1)}, u32[]{:S(2)}) copy-start(f32[1152,128]{1,0:T(8,128)S(1)} %collective-permute-done.left_in) | copy-start | bytes 1769476
  80.9 0.8 copy-start.1

commit v5 on v4

--- a/solution.py
+++ b/solution.py
@@ -72,26 +72,51 @@
     ]
 
 
-def pack_kernel(table, pressure, source, facies, out):
+def tile_span(g):
+    return pl.ds(pl.multiple_of(g * 8, 8), 8)
+
+
+def pack_kernel(table, pressure_in, source_in, facies_in, out, pressure, source, facies, sent, sems):
+    def arrivals(g):
+        pairs = ((pressure_in, pressure), (facies_in, facies), (source_in, source))
+        for k, (there, here) in enumerate(pairs):
+            yield pltpu.make_async_copy(there.at[:, tile_span(g)], here.at[:, tile_span(g)], sems.at[k, g])
+
+    def departure(g):
+        span = pl.ds(g * 128 * HALF, 128 * HALF)
+        return pltpu.make_async_copy(sent.at[span], out.at[span], sems.at[3, g])
+
     def lookup(codes):
         base = jnp.zeros(codes.shape, jnp.float32)
         for code in range(CLASSES):
             base = jnp.where(codes == code, table[code], base)
         return base
 
-    def body(upper, carry):
-        def read(ref):
-            return [ref[upper * GROUP + b] for b in range(GROUP)]
-
-        fields = (read(pressure), [lookup(c) for c in read(facies)], read(source))
-        for k, vectors in enumerate(fields):
-            moved = snake_chunks(exchange(snake_sublanes(vectors)))
-            for b in range(GROUP):
-                row = (32 * ((b >> 1) & 1) + (b >> 2)) * 2 * HALF + (b & 1) * HALF + k * 2 + upper
-                out[pl.ds(row, 8, stride=8 * HALF), :] = moved[b]
+    for g in range(4):
+        for copy in arrivals(g):
+            copy.start()
+
+    def body(g, carry):
+        for copy in arrivals(g):
+            copy.wait()
+        for upper in range(2):
+
+            def read(ref):
+                return [ref[upper * GROUP + b, tile_span(g), :] for b in range(GROUP)]
+
+            fields = (read(pressure), [lookup(c) for c in read(facies)], read(source))
+            for k, vectors in enumerate(fields):
+                moved = snake_chunks(exchange(snake_sublanes(vectors)))
+                for b in range(GROUP):
+                    first = 64 * g + 32 * ((b >> 1) & 1) + (b >> 2)
+                    row = first * 2 * HALF + (b & 1) * HALF + k * 2 + upper
+                    sent[pl.ds(row, 8, stride=8 * HALF), :] = moved[b]
+        departure(g).start()
         return carry
 
-    lax.fori_loop(0, 2, body, 0, unroll=2)
+    lax.fori_loop(0, 4, body, 0)
+    for g in range(4):
+        departure(g).wait()
 
 
 def cell_index():
@@ -423,19 +448,38 @@
         departure(c).wait()
 
 
-def unpack_kernel(recv, pressure, defect):
-    def body(upper, carry):
-        for k, ref in enumerate((pressure, defect)):
-            vectors = []
-            for b in range(GROUP):
-                row = (32 * ((b >> 1) & 1) + (b >> 2)) * 8 + (b & 1) * 4 + k * 2 + upper
-                vectors.append(recv[pl.ds(row, 8, stride=32), :])
-            moved = exchange(snake_sublanes(snake_chunks(vectors)))
-            for b in range(GROUP):
-                ref[upper * GROUP + b] = moved[b]
+def unpack_kernel(recv_in, pressure_out, defect_out, recv, pressure, defect, sems):
+    def arrival(g):
+        span = pl.ds(g * 512, 512)
+        return pltpu.make_async_copy(recv_in.at[span], recv.at[span], sems.at[2, g])
+
+    def departures(g):
+        for k, (here, there) in enumerate(((pressure, pressure_out), (defect, defect_out))):
+            yield pltpu.make_async_copy(here.at[:, tile_span(g)], there.at[:, tile_span(g)], sems.at[k, g])
+
+    for g in range(4):
+        arrival(g).start()
+
+    def body(g, carry):
+        arrival(g).wait()
+        for upper in range(2):
+            for k, ref in enumerate((pressure, defect)):
+                vectors = []
+                for b in range(GROUP):
+                    first = 64 * g + 32 * ((b >> 1) & 1) + (b >> 2)
+                    row = first * 8 + (b & 1) * 4 + k * 2 + upper
+                    vectors.append(recv[pl.ds(row, 8, stride=32), :])
+                moved = exchange(snake_sublanes(snake_chunks(vectors)))
+                for b in range(GROUP):
+                    ref[upper * GROUP + b, tile_span(g), :] = moved[b]
+        for copy in departures(g):
+            copy.start()
         return carry
 
-    lax.fori_loop(0, 2, body, 0, unroll=2)
+    lax.fori_loop(0, 4, body, 0)
+    for g in range(4):
+        for copy in departures(g):
+            copy.wait()
 
 
 def shape(rows):
@@ -449,13 +493,19 @@
 
 def per_device(pressure, source, facies, mobility_table):
     flat = [x.reshape(ROWS, 32, LANES) for x in (pressure, source, facies)]
-    tiles = pl.BlockSpec((ROWS, 8, LANES), lambda g: (0, g, 0))
+    natural = (ROWS, 32, LANES)
     sent = pl.pallas_call(
         pack_kernel,
         out_shape=shape(3072),
-        grid=(4,),
-        in_specs=[SMEM, tiles, tiles, tiles],
-        out_specs=pl.BlockSpec((768, LANES), lambda g: (g, 0)),
+        in_specs=[SMEM, ANY, ANY, ANY],
+        out_specs=ANY,
+        scratch_shapes=[
+            pltpu.VMEM(natural, jnp.float32),
+            pltpu.VMEM(natural, jnp.float32),
+            pltpu.VMEM(natural, jnp.int32),
+            pltpu.VMEM((3072, LANES), jnp.float32),
+            pltpu.SemaphoreType.DMA((4, 4)),
+        ],
         name="pack",
     )(mobility_table, *flat)
     recv = lax.all_to_all(sent.reshape(256, FIELDS, 4, LANES), AXES, 0, 0, tiled=True).reshape(3072, LANES)
@@ -504,10 +554,15 @@
     back = lax.all_to_all(result.reshape(256, 8, LANES), AXES, 0, 0, tiled=True).reshape(2048, LANES)
     outs = pl.pallas_call(
         unpack_kernel,
-        out_shape=(jax.ShapeDtypeStruct((ROWS, 32, LANES), jnp.float32),) * 2,
-        grid=(4,),
-        in_specs=[pl.BlockSpec((512, LANES), lambda g: (g, 0))],
-        out_specs=(tiles, tiles),
+        out_shape=(jax.ShapeDtypeStruct(natural, jnp.float32),) * 2,
+        in_specs=[ANY],
+        out_specs=(ANY, ANY),
+        scratch_shapes=[
+            pltpu.VMEM((2048, LANES), jnp.float32),
+            pltpu.VMEM(natural, jnp.float32),
+            pltpu.VMEM(natural, jnp.float32),
+            pltpu.SemaphoreType.DMA((3, 4)),
+        ],
         name="unpack",
     )(back)
     return tuple(x.reshape(pressure.shape) for x in outs)

time: 145 us -> 144 us (level)
  no operation moved by 1% of the time
where the time goes in v5:
time: 144 us
  blocking collectives  93.6 us (65%)
  Pallas kernels  33.3 us (23%)
  waiting for transfers between devices  9.48 us (7%)
  starting transfers between devices  6.25 us (4%)
    all_to_all x1, blocking collectives, per_device(): lax.all_to_all(sent.reshape(256, FIELDS, 4, LANES), AXES, 0, 0, tiled=True)  57.3 us
    all_to_all x1, blocking collectives, per_device(): lax.all_to_all(result.reshape(256, 8, LANES), AXES, 0, 0, tiled=True)  36.3 us
    pallas_call x1, Pallas kernels, per_device(): pl.pallas_call(work_kernel, out_shape=shape(2048), in_specs=[ANY, ANY, AN...  23.2 us
    ppermute x1, waiting for transfers between devices, per_device(): left_halo = lax.ppermute(upper, AXES, list(zip(chain[:-1], chain[1:])))  5.19 us
    pallas_call x1, Pallas kernels, per_device(): pl.pallas_call(pack_kernel, out_shape=shape(3072), in_specs=[SMEM, ANY, A...  4.44 us
    ppermute x1, starting transfers between devices, per_device(): left_halo = lax.ppermute(upper, AXES, list(zip(chain[:-1], chain[1:])))  4.33 us
    ppermute x1, waiting for transfers between devices, per_device(): right_halo = lax.ppermute(lower, AXES, list(zip(chain[1:], chain[:-1])))  4.29 us
    pallas_call x1, Pallas kernels, per_device(): pl.pallas_call(unpack_kernel, out_shape=(jax.ShapeDtypeStruct(natural, jn...  3.02 us
  transfers between devices with their start and end apart: 2, of which 2 were waited for; matrix products, arithmetic and copies ran while one was open for 0% of the time, Pallas kernels for 0%

profile of v5, /device:TPU:1, one launch (start us, length us, event | category | flops | bytes accessed | tf_op | source)
XLA Modules:
  0.0 144.1 jit_solution(11330921651086233392)
XLA Ops:
  0.6 4.4 %pack.1 = f32[3072,128]{1,0:T(8,128)} custom-call(f32[8]{0:T(128)} %table.1, f32[32,32,128]{2,1,0:T(8,128)} %bitcast.14, f32[32,32,128]{2,1,0:T(8,128)} %bitcast.15, s32[32,32,128]{2,1,0:T(8,128)} %bitcast.16), custom_call_target="tpu_custom_call" | custom-call | tf_op jit(solution)/shard_map/pack/pallas_call | solution.py:497
  5.1 57.3 %all_to_all.10 = f32[256,3,4,128]{3,2,1,0:T(4,128)} all-to-all(f32[256,3,4,128]{3,2,1,0:T(4,128)} %bitcast.11), channel_id=1, replica_groups=mesh['cross'=8,'strike'=32] {'cross','strike'}, dimensions={0} | all-to-all | bytes 3145728 | tf_op jit(solution)/shard_map/all_to_all | solution.py:511
  62.4 2.6 %halves.1 = (f32[1152,128]{1,0:T(8,128)}, f32[1152,128]{1,0:T(8,128)}) custom-call(f32[3072,128]{1,0:T(8,128)} %bitcast.9), custom_call_target="tpu_custom_call" | custom-call | tf_op jit(solution)/shard_map/halves/pallas_call | solution.py:512
  65.0 4.3 %collective-permute-start = (f32[1152,128]{1,0:T(8,128)}, f32[1152,128]{1,0:T(8,128)S(1)}, u32[]{:S(2)}, u32[]{:S(2)}) collective-permute-start(f32[1152,128]{1,0:T(8,128)} %get-tuple-element.6), channel_id=1, source_target_pairs={{0,32},{32,1},{1,33},{33,2},{2,34},{34,3},{3,35},{35,39},{39,7},{7... | collective-permute-start | bytes 1769480 | tf_op jit(solution)/shard_map/ppermute | solution.py:527
  69.4 1.9 %collective-permute-start.1 = (f32[1152,128]{1,0:T(8,128)}, f32[1152,128]{1,0:T(8,128)S(1)}, u32[]{:S(2)}, u32[]{:S(2)}) collective-permute-start(f32[1152,128]{1,0:T(8,128)} %get-tuple-element.7), channel_id=1, source_target_pairs={{32,0},{1,32},{33,1},{2,33},{34,2},{3,34},{35,3},{39,35},{7,39},{3... | collective-permute-start | bytes 1769480 | tf_op jit(solution)/shard_map/ppermute | solution.py:526
  71.3 5.2 %collective-permute-done.left_in = f32[1152,128]{1,0:T(8,128)S(1)} collective-permute-done((f32[1152,128]{1,0:T(8,128)}, f32[1152,128]{1,0:T(8,128)S(1)}, u32[]{:S(2)}, u32[]{:S(2)}) %collective-permute-start) | collective-permute-done | bytes 589856 | tf_op jit(solution)/shard_map/ppermute | solution.py:527
  76.5 0.0 copy-start
  76.5 4.3 %collective-permute-done.1.right_in = f32[1152,128]{1,0:T(8,128)S(1)} collective-permute-done((f32[1152,128]{1,0:T(8,128)}, f32[1152,128]{1,0:T(8,128)S(1)}, u32[]{:S(2)}, u32[]{:S(2)}) %collective-permute-start.1) | collective-permute-done | bytes 589856 | tf_op jit(solution)/shard_map/ppermute | solution.py:526
  80.8 0.0 copy-done
  80.8 0.0 copy-start.1
  80.8 0.8 copy-done.1
  81.6 23.2 %work.1 = f32[2048,128]{1,0:T(8,128)} custom-call(f32[3072,128]{1,0:T(8,128)} %bitcast.10, f32[1152,128]{1,0:T(8,128)} %copy-done, f32[1152,128]{1,0:T(8,128)} %copy-done.1), custom_call_target="tpu_custom_call" | custom-call | tf_op jit(solution)/shard_map/work/pallas_call | solution.py:532
  104.8 36.3 %all_to_all.11 = f32[256,8,128]{2,1,0:T(8,128)} all-to-all(f32[256,8,128]{2,1,0:T(8,128)} %bitcast.13), channel_id=1, replica_groups=mesh['cross'=8,'strike'=32] {'cross','strike'}, dimensions={0} | all-to-all | bytes 2097152 | tf_op jit(solution)/shard_map/all_to_all | solution.py:554
  141.1 3.0 %unpack.1 = (f32[32,32,128]{2,1,0:T(8,128)}, f32[32,32,128]{2,1,0:T(8,128)}) custom-call(f32[2048,128]{1,0:T(8,128)} %bitcast.12), custom_call_target="tpu_custom_call" | custom-call | tf_op jit(solution)/shard_map/unpack/pallas_call | solution.py:555
Async XLA Ops:
  65.0 11.5 %collective-permute-start = (f32[1152,128]{1,0:T(8,128)}, f32[1152,128]{1,0:T(8,128)S(1)}, u32[]{:S(2)}, u32[]{:S(2)}) collective-permute-start(f32[1152,128]{1,0:T(8,128)} %get-tuple-element.6), channel_id=1, source_target_pairs={{0,32},{32,1},{1,33},{33,2},{2,34},{34,3},{3,35},{35,39},{39,7},{7... | collective-permute-start | bytes 1769480 | tf_op jit(solution)/shard_map/ppermute | solution.py:527
  69.4 11.4 %collective-permute-start.1 = (f32[1152,128]{1,0:T(8,128)}, f32[1152,128]{1,0:T(8,128)S(1)}, u32[]{:S(2)}, u32[]{:S(2)}) collective-permute-start(f32[1152,128]{1,0:T(8,128)} %get-tuple-element.7), channel_id=1, source_target_pairs={{32,0},{1,32},{33,1},{2,33},{34,2},{3,34},{35,3},{39,35},{7,39},{3... | collective-permute-start | bytes 1769480 | tf_op jit(solution)/shard_map/ppermute | solution.py:526
  76.5 4.3 %copy-start = (f32[1152,128]{1,0:T(8,128)}, f32[1152,128]{1,0:T(8,128)S(1)}, u32[]{:S(2)}) copy-start(f32[1152,128]{1,0:T(8,128)S(1)} %collective-permute-done.left_in) | copy-start | bytes 1769476
  80.8 0.8 copy-start.1

commit v6 on v5

--- a/solution.py
+++ b/solution.py
@@ -165,7 +165,7 @@
             departure(c, side).start()
         return carry
 
-    lax.fori_loop(0, 8, body, 0)
+    lax.fori_loop(0, 8, body, 0, unroll=2)
     for c in range(8):
         for side in range(2):
             departure(c, side).wait()
@@ -276,7 +276,7 @@
             power[i] = value
             return value * ratio
 
-        block_ratio = lax.fori_loop(0, ROWS, powers, jnp.ones(SLAB, jnp.float32), unroll=2)
+        block_ratio = lax.fori_loop(0, ROWS, powers, jnp.ones(SLAB, jnp.float32), unroll=4)
         power[ROWS] = block_ratio
         squares = [block_ratio]
         for _ in range(5):

time: 144 us -> 144 us (level)
  no operation moved by 1% of the time
where the time goes in v6:
time: 144 us
  blocking collectives  93.6 us (65%)
  Pallas kernels  33.2 us (23%)
  waiting for transfers between devices  9.48 us (7%)
  starting transfers between devices  6.25 us (4%)
    all_to_all x1, blocking collectives, per_device(): lax.all_to_all(sent.reshape(256, FIELDS, 4, LANES), AXES, 0, 0, tiled=True)  57.3 us
    all_to_all x1, blocking collectives, per_device(): lax.all_to_all(result.reshape(256, 8, LANES), AXES, 0, 0, tiled=True)  36.3 us
    pallas_call x1, Pallas kernels, per_device(): pl.pallas_call(work_kernel, out_shape=shape(2048), in_specs=[ANY, ANY, AN...  23.1 us
    ppermute x1, waiting for transfers between devices, per_device(): left_halo = lax.ppermute(upper, AXES, list(zip(chain[:-1], chain[1:])))  5.19 us
    pallas_call x1, Pallas kernels, per_device(): pl.pallas_call(pack_kernel, out_shape=shape(3072), in_specs=[SMEM, ANY, A...  4.44 us
    ppermute x1, starting transfers between devices, per_device(): left_halo = lax.ppermute(upper, AXES, list(zip(chain[:-1], chain[1:])))  4.33 us
    ppermute x1, waiting for transfers between devices, per_device(): right_halo = lax.ppermute(lower, AXES, list(zip(chain[1:], chain[:-1])))  4.29 us
    pallas_call x1, Pallas kernels, per_device(): pl.pallas_call(unpack_kernel, out_shape=(jax.ShapeDtypeStruct(natural, jn...  3.02 us
  transfers between devices with their start and end apart: 2, of which 2 were waited for; matrix products, arithmetic and copies ran while one was open for 0% of the time, Pallas kernels for 0%

profile of v6, /device:TPU:1, one launch (start us, length us, event | category | flops | bytes accessed | tf_op | source)
XLA Modules:
  0.0 144.1 jit_solution(9243332759385068887)
XLA Ops:
  0.6 4.4 %pack.1 = f32[3072,128]{1,0:T(8,128)} custom-call(f32[8]{0:T(128)} %table.1, f32[32,32,128]{2,1,0:T(8,128)} %bitcast.14, f32[32,32,128]{2,1,0:T(8,128)} %bitcast.15, s32[32,32,128]{2,1,0:T(8,128)} %bitcast.16), custom_call_target="tpu_custom_call" | custom-call | tf_op jit(solution)/shard_map/pack/pallas_call | solution.py:497
  5.1 57.3 %all_to_all.10 = f32[256,3,4,128]{3,2,1,0:T(4,128)} all-to-all(f32[256,3,4,128]{3,2,1,0:T(4,128)} %bitcast.11), channel_id=1, replica_groups=mesh['cross'=8,'strike'=32] {'cross','strike'}, dimensions={0} | all-to-all | bytes 3145728 | tf_op jit(solution)/shard_map/all_to_all | solution.py:511
  62.4 2.6 %halves.1 = (f32[1152,128]{1,0:T(8,128)}, f32[1152,128]{1,0:T(8,128)}) custom-call(f32[3072,128]{1,0:T(8,128)} %bitcast.9), custom_call_target="tpu_custom_call" | custom-call | tf_op jit(solution)/shard_map/halves/pallas_call | solution.py:512
  65.0 4.3 %collective-permute-start = (f32[1152,128]{1,0:T(8,128)}, f32[1152,128]{1,0:T(8,128)S(1)}, u32[]{:S(2)}, u32[]{:S(2)}) collective-permute-start(f32[1152,128]{1,0:T(8,128)} %get-tuple-element.6), channel_id=1, source_target_pairs={{0,32},{32,1},{1,33},{33,2},{2,34},{34,3},{3,35},{35,39},{39,7},{7... | collective-permute-start | bytes 1769480 | tf_op jit(solution)/shard_map/ppermute | solution.py:527
  69.4 1.9 %collective-permute-start.1 = (f32[1152,128]{1,0:T(8,128)}, f32[1152,128]{1,0:T(8,128)S(1)}, u32[]{:S(2)}, u32[]{:S(2)}) collective-permute-start(f32[1152,128]{1,0:T(8,128)} %get-tuple-element.7), channel_id=1, source_target_pairs={{32,0},{1,32},{33,1},{2,33},{34,2},{3,34},{35,3},{39,35},{7,39},{3... | collective-permute-start | bytes 1769480 | tf_op jit(solution)/shard_map/ppermute | solution.py:526
  71.3 5.2 %collective-permute-done.left_in = f32[1152,128]{1,0:T(8,128)S(1)} collective-permute-done((f32[1152,128]{1,0:T(8,128)}, f32[1152,128]{1,0:T(8,128)S(1)}, u32[]{:S(2)}, u32[]{:S(2)}) %collective-permute-start) | collective-permute-done | bytes 589856 | tf_op jit(solution)/shard_map/ppermute | solution.py:527
  76.5 0.0 copy-start
  76.5 4.3 %collective-permute-done.1.right_in = f32[1152,128]{1,0:T(8,128)S(1)} collective-permute-done((f32[1152,128]{1,0:T(8,128)}, f32[1152,128]{1,0:T(8,128)S(1)}, u32[]{:S(2)}, u32[]{:S(2)}) %collective-permute-start.1) | collective-permute-done | bytes 589856 | tf_op jit(solution)/shard_map/ppermute | solution.py:526
  80.8 0.0 copy-done
  80.8 0.0 copy-start.1
  80.8 0.8 copy-done.1
  81.6 23.1 %work.1 = f32[2048,128]{1,0:T(8,128)} custom-call(f32[3072,128]{1,0:T(8,128)} %bitcast.10, f32[1152,128]{1,0:T(8,128)} %copy-done, f32[1152,128]{1,0:T(8,128)} %copy-done.1), custom_call_target="tpu_custom_call" | custom-call | tf_op jit(solution)/shard_map/work/pallas_call | solution.py:532
  104.7 36.3 %all_to_all.11 = f32[256,8,128]{2,1,0:T(8,128)} all-to-all(f32[256,8,128]{2,1,0:T(8,128)} %bitcast.13), channel_id=1, replica_groups=mesh['cross'=8,'strike'=32] {'cross','strike'}, dimensions={0} | all-to-all | bytes 2097152 | tf_op jit(solution)/shard_map/all_to_all | solution.py:554
  141.0 3.0 %unpack.1 = (f32[32,32,128]{2,1,0:T(8,128)}, f32[32,32,128]{2,1,0:T(8,128)}) custom-call(f32[2048,128]{1,0:T(8,128)} %bitcast.12), custom_call_target="tpu_custom_call" | custom-call | tf_op jit(solution)/shard_map/unpack/pallas_call | solution.py:555
Async XLA Ops:
  65.0 11.5 %collective-permute-start = (f32[1152,128]{1,0:T(8,128)}, f32[1152,128]{1,0:T(8,128)S(1)}, u32[]{:S(2)}, u32[]{:S(2)}) collective-permute-start(f32[1152,128]{1,0:T(8,128)} %get-tuple-element.6), channel_id=1, source_target_pairs={{0,32},{32,1},{1,33},{33,2},{2,34},{34,3},{3,35},{35,39},{39,7},{7... | collective-permute-start | bytes 1769480 | tf_op jit(solution)/shard_map/ppermute | solution.py:527
  69.4 11.4 %collective-permute-start.1 = (f32[1152,128]{1,0:T(8,128)}, f32[1152,128]{1,0:T(8,128)S(1)}, u32[]{:S(2)}, u32[]{:S(2)}) collective-permute-start(f32[1152,128]{1,0:T(8,128)} %get-tuple-element.7), channel_id=1, source_target_pairs={{32,0},{1,32},{33,1},{2,33},{34,2},{3,34},{35,3},{39,35},{7,39},{3... | collective-permute-start | bytes 1769480 | tf_op jit(solution)/shard_map/ppermute | solution.py:526
  76.5 4.3 %copy-start = (f32[1152,128]{1,0:T(8,128)}, f32[1152,128]{1,0:T(8,128)S(1)}, u32[]{:S(2)}) copy-start(f32[1152,128]{1,0:T(8,128)S(1)} %collective-permute-done.left_in) | copy-start | bytes 1769476
  80.8 0.8 copy-start.1
